TPU v7x, 128 devices: a whole 4x4x4 slice. The times are simulated.
128 devices in a mesh: cube: 16 (over z, y), front: 8 (over x, core).
Axes of the slice: x: 4, y: 4, z: 4, core: 2. Of those that a mesh axis runs over, the one named last changes fastest.
Arguments:
- parent_front: float32 [16384, 16384], P('cube', 'front'), as said below
- child_entries: float32 [16384, 8192], P('cube', 'front'), as said below
- child_index: int32 [2, 64], replicated, may hold values from 0 to 127, as said below
Outputs:
- factor: float32 [16384, 16384], P('cube', 'front')
Inputs may be any that keep to these rules, and one draw needn't show every extreme that they name: parent_front, taken to the front's order, is symmetric positive definite. `child_entries`: each child's contribution block is symmetric positive semidefinite. For each child s the entries child_index[s, b] are distinct parent block numbers. Within each aligned run of 8 entries of one child no two are equal modulo 16, and each remainder modulo 8 occurs exactly once in it.
All inputs are finite; a program needn't handle non-finite values.
Results may differ from a plain program's by a relative error of at most 0.000059.
Values sent between devices are 32-bit elements; how exact they have to be, the bound alone decides.
No kernel may reach another device: no remote copies, remote signals or barrier semaphores. Data moves between devices by JAX's collectives and lax.ppermute only.
A program may use at most 128 MiB of HBM per device.

v0:
```python
import jax
import jax.numpy as jnp
from jax import lax
from jax.sharding import PartitionSpec as P

BLK = 128
NPB = 6


EXACT = lax.Precision.HIGHEST


def spread_2(block, axis, owner):
    block = jnp.where(lax.axis_index(axis) == owner, block, jnp.zeros_like(block))
    return lax.psum(block, axis)


def body(parent_front, child_entries, child_index):
    n_cube = lax.axis_size("cube")
    n_front = lax.axis_size("front")
    cube_pos = lax.axis_index("cube")
    front_pos = lax.axis_index("front")
    row_count, col_count = parent_front.shape
    row_blocks = row_count // BLK
    col_blocks = col_count // BLK
    tier_count = n_cube // n_front
    groups = n_cube // 2
    child_rows = child_entries.shape[0]
    child_cols = child_entries.shape[1] // BLK
    per_front = child_cols // n_front
    own_child = cube_pos // groups
    own_group = cube_pos % groups
    own_list = lax.dynamic_index_in_dim(child_index, own_child, 0, keepdims=False)
    row_targets = lax.dynamic_slice_in_dim(own_list, own_group * row_blocks, row_blocks)
    col_targets = lax.dynamic_slice_in_dim(own_list, front_pos * child_cols, child_cols)
    order_key = col_targets % n_front * child_cols + jnp.arange(child_cols, dtype=jnp.int32)
    col_order = jnp.argsort(order_key)
    tile_set = jnp.take(child_entries.reshape(child_rows, child_cols, BLK), col_order, axis=1)
    tile_set = tile_set.reshape(row_blocks, BLK, n_front, per_front, BLK)
    owners = row_targets % n_cube
    to_owner = (owners[None, :] == jnp.arange(n_cube, dtype=jnp.int32)[:, None]).astype(jnp.float32)
    outgoing = jnp.einsum("ou,uxfty->ofxty", to_owner, tile_set, precision=EXACT)
    flat_tiles = outgoing.reshape((n_cube * n_front,) + outgoing.shape[2:])
    arrived = lax.all_to_all(
        flat_tiles, ("cube", "front"), split_axis=0, concat_axis=0, tiled=True
    ).reshape(outgoing.shape)
    layout = "gfxty"
    assembled = parent_front
    for child_id in range(2):
        child_list = child_index[child_id]
        by_group = child_list.reshape(groups, row_blocks)
        is_mine = by_group % n_cube == cube_pos
        local_row = by_group // n_cube
        row_hits = is_mine[:, :, None] & (
            local_row[:, :, None] == jnp.arange(row_blocks, dtype=jnp.int32)[None, None, :]
        )
        row_map = jnp.sum(row_hits.astype(jnp.float32), axis=1)
        by_front = child_list.reshape(n_front, child_cols)
        is_match = by_front % n_front == front_pos
        match_int = is_match.astype(jnp.int32)
        col_rank = jnp.cumsum(match_int, axis=1) - match_int
        local_col = by_front // n_front
        col_hits = is_match[:, :, None, None] & (
            col_rank[:, :, None, None]
            == jnp.arange(per_front, dtype=jnp.int32)[None, None, :, None]
        )
        col_hits = col_hits & (
            local_col[:, :, None, None]
            == jnp.arange(col_blocks, dtype=jnp.int32)[None, None, None, :]
        )
        col_map = jnp.sum(col_hits.astype(jnp.float32), axis=1)
        received = lax.slice_in_dim(arrived, child_id * groups, (child_id + 1) * groups, axis=0)
        spread = jnp.einsum("gi," + layout + "->ixfty", row_map, received, precision=EXACT)
        placed = jnp.einsum("ixfty,ftk->ixky", spread, col_map, precision=EXACT)
        assembled = assembled + placed.reshape(row_count, col_count)
    row_pivots = cube_pos + n_cube * jnp.arange(row_blocks, dtype=jnp.int32)
    col_pivots = front_pos + n_front * jnp.arange(col_blocks, dtype=jnp.int32)
    row_ids = jnp.repeat(row_pivots, BLK)
    eye_block = jnp.eye(BLK, dtype=jnp.float32)

    def panel_info(matrix, pivot):
        root_cube = pivot % n_cube
        root_front = pivot % n_front
        row_at = pivot // n_cube
        col_at = pivot // n_front
        corner = lax.dynamic_slice(matrix, (row_at * BLK, col_at * BLK), (BLK, BLK))
        corner = spread_2(corner, "cube", root_cube)
        corner = jnp.where(front_pos == root_front, corner, eye_block)
        diag_factor = jnp.linalg.cholesky(corner)
        inverse = jax.scipy.linalg.solve_triangular(diag_factor, eye_block, lower=True)
        column = lax.dynamic_slice_in_dim(matrix, col_at * BLK, BLK, axis=1)
        panel = jnp.dot(column, inverse.T, precision=EXACT)
        panel = jnp.where(row_ids[:, None] > pivot, panel, 0.0)
        panel = jnp.where(row_ids[:, None] == pivot, jnp.tile(diag_factor, (row_blocks, 1)), panel)
        row_panel = spread_2(panel, "front", root_front)
        pieces = []
        for tier in range(tier_count):
            pieces.append(
                spread_2(row_panel, "cube", front_pos + n_front * tier).reshape(
                    row_blocks, BLK, BLK
                )
            )
        col_panel = jnp.stack(pieces, axis=1).reshape(col_count, BLK)
        return (row_panel, col_panel)

    def apply_step(matrix, pivot_ids, panel_part, pivot, row_panel):
        width = pivot_ids.shape[0]
        product = jnp.dot(row_panel, panel_part.T, precision=EXACT).reshape(row_count, width, BLK)
        current = matrix.reshape(row_count, width, BLK)
        row_ref = row_ids[:, None, None]
        col_ref = pivot_ids[None, :, None]
        result = jnp.where((row_ref > pivot) & (col_ref > pivot), current - product, current)
        result = jnp.where((row_ref == pivot) & (col_ref > pivot), 0.0, result)
        result = jnp.where((col_ref == pivot) & (row_ref >= pivot), row_panel[:, None, :], result)
        return result.reshape(row_count, width * BLK)

    def advance(pivot, matrix):
        row_panel, col_panel = panel_info(matrix, pivot)
        return apply_step(matrix, col_pivots, col_panel, pivot, row_panel)

    finished = lax.fori_loop(0, NPB, advance, assembled)
    return finished


def solution(mesh):
    placed = (P("cube", "front"), P("cube", "front"), P())
    return jax.shard_map(
        body, mesh=mesh, in_specs=placed, out_specs=P("cube", "front"), check_vma=False
    )
```

profile of v0, /device:TPU:0, one launch (start us, length us, event | category | flops | bytes accessed | tf_op | source)
XLA Modules:
  0.0 1971.5 jit_solution(7263421743182237402)
XLA Ops:
  38.7 19.0 copy.74
  79.7 88.6 %all-to-all-done = f32[128,128,1,128]{3,1,2,0:T(8,128)} async-done(((f32[128,128,1,128]{3,1,2,0:T(8,128)}), f32[128,128,1,128]{3,1,2,0:T(8,128)}, u32[]{:S(2)}, u32[]{:S(2)}) %all-to-all-start) | async-done | bytes 8388640 | tf_op jit(solution)/shard_map/all_to_all | solution.py:44
  241.0 13.6 add_add_fusion
  254.7 1700.5 %while.19 = (s32[]{:T(128)}, f32[1024,2048]{0,1:T(8,128)}, s32[]{:T(128)}, s32[]{:T(128)}, s32[8]{0:T(128)S(1)}, /*index=5*/s32[]{:T(128)}, s32[]{:T(128)}, s32[...) while((s32[]{:T(128)}, f32[1024,2048]{0,1:T(8,128)}, ...), condition=%wide.region_14.15_spmd.clone.clone.clone, body=%wide.region_7.14_spmd.clone.clone.clone.sunk | while | flops 3457777920 | bytes 57714556 | solution.py:121
  265.7 85.2 %all-reduce.7.cloned.1.call-done = f32[128,128]{1,0:T(8,128)} async-done(((f32[128,128]{1,0:T(8,128)}), f32[128,128]{1,0:T(8,128)}) %all-reduce.7.cloned.1.call-update) | async-done | bytes 65552 | tf_op jit(solution)/shard_map/while/body/eval_jaxpr/psum | solution.py:15
  379.1 58.6 %all-reduce.9.cloned.1.call-done = f32[1024,128]{1,0:T(8,128)} async-done(((f32[1024,128]{1,0:T(8,128)}), f32[1024,128]{1,0:T(8,128)}) %all-reduce.9.cloned.1.call-update) | async-done | bytes 524304 | tf_op jit(solution)/shard_map/while/body/eval_jaxpr/psum | solution.py:15
  441.4 86.3 %all-reduce.11.cloned.1.call-done = (f32[8,1,128,128]{3,2,0,1:T(8,128)}, f32[8,1,128,128]{3,2,0,1:T(8,128)}) async-done(((f32[8,1,128,128]{3,2,0,1:T(8,128)}, f32[8,1,128,128]{3,2,0,1:T(8,128)}), (f32[8,1,128,128]{3,2,0,1:T(8,128)}, f32[8,1,128,128]{3,2,0,1:T(8,128)})) %all-reduce.11.cloned.1.call-update) | async-done | bytes 1048592 | tf_op jit(solution)/shard_map/while/body/eval_jaxpr/psum | solution.py:15
  529.1 12.1 fusion.92
  552.0 81.4 %all-reduce.7.cloned.1.call-done = f32[128,128]{1,0:T(8,128)} async-done(((f32[128,128]{1,0:T(8,128)}), f32[128,128]{1,0:T(8,128)}) %all-reduce.7.cloned.1.call-update) | async-done | bytes 65552 | tf_op jit(solution)/shard_map/while/body/eval_jaxpr/psum | solution.py:15
  659.8 60.4 %all-reduce.9.cloned.1.call-done = f32[1024,128]{1,0:T(8,128)} async-done(((f32[1024,128]{1,0:T(8,128)}), f32[1024,128]{1,0:T(8,128)}) %all-reduce.9.cloned.1.call-update) | async-done | bytes 524304 | tf_op jit(solution)/shard_map/while/body/eval_jaxpr/psum | solution.py:15
  723.9 86.2 %all-reduce.11.cloned.1.call-done = (f32[8,1,128,128]{3,2,0,1:T(8,128)}, f32[8,1,128,128]{3,2,0,1:T(8,128)}) async-done(((f32[8,1,128,128]{3,2,0,1:T(8,128)}, f32[8,1,128,128]{3,2,0,1:T(8,128)}), (f32[8,1,128,128]{3,2,0,1:T(8,128)}, f32[8,1,128,128]{3,2,0,1:T(8,128)})) %all-reduce.11.cloned.1.call-update) | async-done | bytes 1048592 | tf_op jit(solution)/shard_map/while/body/eval_jaxpr/psum | solution.py:15
  811.5 12.1 fusion.92
  834.4 81.4 %all-reduce.7.cloned.1.call-done = f32[128,128]{1,0:T(8,128)} async-done(((f32[128,128]{1,0:T(8,128)}), f32[128,128]{1,0:T(8,128)}) %all-reduce.7.cloned.1.call-update) | async-done | bytes 65552 | tf_op jit(solution)/shard_map/while/body/eval_jaxpr/psum | solution.py:15
  942.2 60.5 %all-reduce.9.cloned.1.call-done = f32[1024,128]{1,0:T(8,128)} async-done(((f32[1024,128]{1,0:T(8,128)}), f32[1024,128]{1,0:T(8,128)}) %all-reduce.9.cloned.1.call-update) | async-done | bytes 524304 | tf_op jit(solution)/shard_map/while/body/eval_jaxpr/psum | solution.py:15
  1006.4 86.4 %all-reduce.11.cloned.1.call-done = (f32[8,1,128,128]{3,2,0,1:T(8,128)}, f32[8,1,128,128]{3,2,0,1:T(8,128)}) async-done(((f32[8,1,128,128]{3,2,0,1:T(8,128)}, f32[8,1,128,128]{3,2,0,1:T(8,128)}), (f32[8,1,128,128]{3,2,0,1:T(8,128)}, f32[8,1,128,128]{3,2,0,1:T(8,128)})) %all-reduce.11.cloned.1.call-update) | async-done | bytes 1048592 | tf_op jit(solution)/shard_map/while/body/eval_jaxpr/psum | solution.py:15
  1117.1 81.4 %all-reduce.7.cloned.1.call-done = f32[128,128]{1,0:T(8,128)} async-done(((f32[128,128]{1,0:T(8,128)}), f32[128,128]{1,0:T(8,128)}) %all-reduce.7.cloned.1.call-update) | async-done | bytes 65552 | tf_op jit(solution)/shard_map/while/body/eval_jaxpr/psum | solution.py:15
  1224.9 60.4 %all-reduce.9.cloned.1.call-done = f32[1024,128]{1,0:T(8,128)} async-done(((f32[1024,128]{1,0:T(8,128)}), f32[1024,128]{1,0:T(8,128)}) %all-reduce.9.cloned.1.call-update) | async-done | bytes 524304 | tf_op jit(solution)/shard_map/while/body/eval_jaxpr/psum | solution.py:15
  1289.0 86.2 %all-reduce.11.cloned.1.call-done = (f32[8,1,128,128]{3,2,0,1:T(8,128)}, f32[8,1,128,128]{3,2,0,1:T(8,128)}) async-done(((f32[8,1,128,128]{3,2,0,1:T(8,128)}, f32[8,1,128,128]{3,2,0,1:T(8,128)}), (f32[8,1,128,128]{3,2,0,1:T(8,128)}, f32[8,1,128,128]{3,2,0,1:T(8,128)})) %all-reduce.11.cloned.1.call-update) | async-done | bytes 1048592 | tf_op jit(solution)/shard_map/while/body/eval_jaxpr/psum | solution.py:15
  1399.5 81.4 %all-reduce.7.cloned.1.call-done = f32[128,128]{1,0:T(8,128)} async-done(((f32[128,128]{1,0:T(8,128)}), f32[128,128]{1,0:T(8,128)}) %all-reduce.7.cloned.1.call-update) | async-done | bytes 65552 | tf_op jit(solution)/shard_map/while/body/eval_jaxpr/psum | solution.py:15
  1507.3 62.0 %all-reduce.9.cloned.1.call-done = f32[1024,128]{1,0:T(8,128)} async-done(((f32[1024,128]{1,0:T(8,128)}), f32[1024,128]{1,0:T(8,128)}) %all-reduce.9.cloned.1.call-update) | async-done | bytes 524304 | tf_op jit(solution)/shard_map/while/body/eval_jaxpr/psum | solution.py:15
  1573.1 86.2 %all-reduce.11.cloned.1.call-done = (f32[8,1,128,128]{3,2,0,1:T(8,128)}, f32[8,1,128,128]{3,2,0,1:T(8,128)}) async-done(((f32[8,1,128,128]{3,2,0,1:T(8,128)}, f32[8,1,128,128]{3,2,0,1:T(8,128)}), (f32[8,1,128,128]{3,2,0,1:T(8,128)}, f32[8,1,128,128]{3,2,0,1:T(8,128)})) %all-reduce.11.cloned.1.call-update) | async-done | bytes 1048592 | tf_op jit(solution)/shard_map/while/body/eval_jaxpr/psum | solution.py:15
  1683.5 81.4 %all-reduce.7.cloned.1.call-done = f32[128,128]{1,0:T(8,128)} async-done(((f32[128,128]{1,0:T(8,128)}), f32[128,128]{1,0:T(8,128)}) %all-reduce.7.cloned.1.call-update) | async-done | bytes 65552 | tf_op jit(solution)/shard_map/while/body/eval_jaxpr/psum | solution.py:15
  1791.4 60.4 %all-reduce.9.cloned.1.call-done = f32[1024,128]{1,0:T(8,128)} async-done(((f32[1024,128]{1,0:T(8,128)}), f32[1024,128]{1,0:T(8,128)}) %all-reduce.9.cloned.1.call-update) | async-done | bytes 524304 | tf_op jit(solution)/shard_map/while/body/eval_jaxpr/psum | solution.py:15
  1855.4 86.2 %all-reduce.11.cloned.1.call-done = (f32[8,1,128,128]{3,2,0,1:T(8,128)}, f32[8,1,128,128]{3,2,0,1:T(8,128)}) async-done(((f32[8,1,128,128]{3,2,0,1:T(8,128)}, f32[8,1,128,128]{3,2,0,1:T(8,128)}), (f32[8,1,128,128]{3,2,0,1:T(8,128)}, f32[8,1,128,128]{3,2,0,1:T(8,128)})) %all-reduce.11.cloned.1.call-update) | async-done | bytes 1048592 | tf_op jit(solution)/shard_map/while/body/eval_jaxpr/psum | solution.py:15
  (232 shorter events, 438.9 us)
Async XLA Ops:
  57.7 110.6 %all-to-all-start = ((f32[128,128,1,128]{3,1,2,0:T(8,128)}), f32[128,128,1,128]{3,1,2,0:T(8,128)}, u32[]{:S(2)}, u32[]{:S(2)}) async-start(f32[128,128,1,128]{3,1,2,0:T(8,128)} %bitcast.123), calls=%async_computation | async-start | bytes 16777216 | tf_op jit(solution)/shard_map/all_to_all | solution.py:44
  254.9 96.1 %all-reduce.7.cloned.1.call-start = ((), (), s32[]{:S(2)}) async-start(), calls=%async_computation.1 | async-start | bytes 131072 | tf_op jit(solution)/shard_map/while/body/eval_jaxpr/psum | solution.py:15
  265.6 172.1 %all-reduce.9.cloned.1.call-start = ((), (), s32[]{:S(2)}) async-start(), calls=%async_computation.2 | async-start | bytes 1048576 | tf_op jit(solution)/shard_map/while/body/eval_jaxpr/psum | solution.py:15
  379.0 148.7 %all-reduce.11.cloned.1.call-start = ((), (), s32[]{:S(2)}) async-start(), calls=%async_computation.3 | async-start | bytes 2097152 | tf_op jit(solution)/shard_map/while/body/eval_jaxpr/psum | solution.py:15
  437.7 91.4 %copy-start = (f32[1024,128]{1,0:T(8,128)S(1)}, f32[1024,128]{1,0:T(8,128)}, u32[]{:S(2)}) copy-start(f32[1024,128]{1,0:T(8,128)} %all-reduce.9.cloned.1.call-done) | copy-start | bytes 1572868 | tf_op jit(solution)/shard_map/while
  541.2 92.1 %all-reduce.7.cloned.1.call-start = ((), (), s32[]{:S(2)}) async-start(), calls=%async_computation.1 | async-start | bytes 131072 | tf_op jit(solution)/shard_map/while/body/eval_jaxpr/psum | solution.py:15
  551.9 168.4 %all-reduce.9.cloned.1.call-start = ((), (), s32[]{:S(2)}) async-start(), calls=%async_computation.2 | async-start | bytes 1048576 | tf_op jit(solution)/shard_map/while/body/eval_jaxpr/psum | solution.py:15
  659.8 150.3 %all-reduce.11.cloned.1.call-start = ((), (), s32[]{:S(2)}) async-start(), calls=%async_computation.3 | async-start | bytes 2097152 | tf_op jit(solution)/shard_map/while/body/eval_jaxpr/psum | solution.py:15
  720.2 91.3 %copy-start = (f32[1024,128]{1,0:T(8,128)S(1)}, f32[1024,128]{1,0:T(8,128)}, u32[]{:S(2)}) copy-start(f32[1024,128]{1,0:T(8,128)} %all-reduce.9.cloned.1.call-done) | copy-start | bytes 1572868 | tf_op jit(solution)/shard_map/while
  823.6 92.1 %all-reduce.7.cloned.1.call-start = ((), (), s32[]{:S(2)}) async-start(), calls=%async_computation.1 | async-start | bytes 131072 | tf_op jit(solution)/shard_map/while/body/eval_jaxpr/psum | solution.py:15
  834.2 168.5 %all-reduce.9.cloned.1.call-start = ((), (), s32[]{:S(2)}) async-start(), calls=%async_computation.2 | async-start | bytes 1048576 | tf_op jit(solution)/shard_map/while/body/eval_jaxpr/psum | solution.py:15
  942.2 150.7 %all-reduce.11.cloned.1.call-start = ((), (), s32[]{:S(2)}) async-start(), calls=%async_computation.3 | async-start | bytes 2097152 | tf_op jit(solution)/shard_map/while/body/eval_jaxpr/psum | solution.py:15
  1002.7 91.5 %copy-start = (f32[1024,128]{1,0:T(8,128)S(1)}, f32[1024,128]{1,0:T(8,128)}, u32[]{:S(2)}) copy-start(f32[1024,128]{1,0:T(8,128)} %all-reduce.9.cloned.1.call-done) | copy-start | bytes 1572868 | tf_op jit(solution)/shard_map/while
  1106.3 92.1 %all-reduce.7.cloned.1.call-start = ((), (), s32[]{:S(2)}) async-start(), calls=%async_computation.1 | async-start | bytes 131072 | tf_op jit(solution)/shard_map/while/body/eval_jaxpr/psum | solution.py:15
  1117.0 168.4 %all-reduce.9.cloned.1.call-start = ((), (), s32[]{:S(2)}) async-start(), calls=%async_computation.2 | async-start | bytes 1048576 | tf_op jit(solution)/shard_map/while/body/eval_jaxpr/psum | solution.py:15
  1224.9 150.3 %all-reduce.11.cloned.1.call-start = ((), (), s32[]{:S(2)}) async-start(), calls=%async_computation.3 | async-start | bytes 2097152 | tf_op jit(solution)/shard_map/while/body/eval_jaxpr/psum | solution.py:15
  1285.3 91.3 %copy-start = (f32[1024,128]{1,0:T(8,128)S(1)}, f32[1024,128]{1,0:T(8,128)}, u32[]{:S(2)}) copy-start(f32[1024,128]{1,0:T(8,128)} %all-reduce.9.cloned.1.call-done) | copy-start | bytes 1572868 | tf_op jit(solution)/shard_map/while
  1388.7 92.1 %all-reduce.7.cloned.1.call-start = ((), (), s32[]{:S(2)}) async-start(), calls=%async_computation.1 | async-start | bytes 131072 | tf_op jit(solution)/shard_map/while/body/eval_jaxpr/psum | solution.py:15
  1399.3 170.0 %all-reduce.9.cloned.1.call-start = ((), (), s32[]{:S(2)}) async-start(), calls=%async_computation.2 | async-start | bytes 1048576 | tf_op jit(solution)/shard_map/while/body/eval_jaxpr/psum | solution.py:15
  1507.3 152.0 %all-reduce.11.cloned.1.call-start = ((), (), s32[]{:S(2)}) async-start(), calls=%async_computation.3 | async-start | bytes 2097152 | tf_op jit(solution)/shard_map/while/body/eval_jaxpr/psum | solution.py:15
  1672.8 92.1 %all-reduce.7.cloned.1.call-start = ((), (), s32[]{:S(2)}) async-start(), calls=%async_computation.1 | async-start | bytes 131072 | tf_op jit(solution)/shard_map/while/body/eval_jaxpr/psum | solution.py:15
  1683.4 168.4 %all-reduce.9.cloned.1.call-start = ((), (), s32[]{:S(2)}) async-start(), calls=%async_computation.2 | async-start | bytes 1048576 | tf_op jit(solution)/shard_map/while/body/eval_jaxpr/psum | solution.py:15
  1791.3 150.3 %all-reduce.11.cloned.1.call-start = ((), (), s32[]{:S(2)}) async-start(), calls=%async_computation.3 | async-start | bytes 2097152 | tf_op jit(solution)/shard_map/while/body/eval_jaxpr/psum | solution.py:15
  1851.7 91.3 %copy-start = (f32[1024,128]{1,0:T(8,128)S(1)}, f32[1024,128]{1,0:T(8,128)}, u32[]{:S(2)}) copy-start(f32[1024,128]{1,0:T(8,128)} %all-reduce.9.cloned.1.call-done) | copy-start | bytes 1572868 | tf_op jit(solution)/shard_map/while
  (2 other events, 97.8 us)
Sparse Core Ops, SparseCore 0:
  265.7 85.1 all-reduce.6
  379.1 58.4 all-reduce.8
  441.0 86.6 all-reduce.10
  552.0 81.3 all-reduce.6
  659.9 60.2 all-reduce.8
  723.4 86.6 all-reduce.10
  834.4 81.3 all-reduce.6
  942.3 60.4 all-reduce.8
  1006.1 86.6 all-reduce.10
  1117.1 81.3 all-reduce.6
  1225.0 60.2 all-reduce.8
  1288.5 86.6 all-reduce.10
  1399.5 81.3 all-reduce.6
  1507.4 61.9 all-reduce.8
  1572.5 86.6 all-reduce.10
  1683.5 81.3 all-reduce.6
  1791.4 60.2 all-reduce.8
  1854.9 86.6 all-reduce.10
where the time goes:
time: 1980 us; the launch traced here: 1970 us
  waiting for transfers between devices  1460 us (74%)
  other arithmetic  188 us (9%)
  local copies, waits for them, and re-layouts  164 us (8%)
  matrix products  131 us (7%)
    psum x18, waiting for transfers between devices, spread_2(): return lax.psum(block, axis)  1370 us
    all_to_all x1, waiting for transfers between devices, body(): lax.all_to_all(flat_tiles, ('cube', 'front'), split_axis=0, concat_axis=0...  88.6 us
    another operation x18, other arithmetic, panel_info(): diag_factor = jnp.linalg.cholesky(corner)  74.3 us
    dot_general x6, matrix products, apply_step(): jnp.dot(row_panel, panel_part.T, precision=EXACT)  72.8 us
    another operation x12, other arithmetic, panel_info(): jax.scipy.linalg.solve_triangular(diag_factor, eye_block, lower=True)  62.8 us
    while x18, local copies, waits for them, and re-layouts  54.8 us
  transfers between devices with their start and end apart: 19, of which 19 were waited for; matrix products, arithmetic and copies ran while one was open for 1% of the time, Pallas kernels for 0%

commit v1 on v0

v1 whole, which is shorter than its diff:
```python
import functools

import jax
import jax.numpy as jnp
from jax import lax
from jax.experimental import pallas as pl
from jax.experimental.pallas import tpu as pltpu
from jax.sharding import Mesh, PartitionSpec as P

BLK = 128
NPB = 6
NPIV = NPB * BLK
SUB = 8

EXACT = lax.Precision.HIGHEST
F32 = jnp.float32
CUBE = ("half", "res")
VMEM_LIMIT = 56 * 1024 * 1024


def find(idx_ref, base, residue):
    place = jnp.int32(0)
    for u in range(8):
        place = place + jnp.where(lax.rem(idx_ref[base + u], 8) == residue, u, 0)
    return place


def params():
    return pltpu.CompilerParams(vmem_limit_bytes=VMEM_LIMIT)


def pack_kernel(idx_ref, pos_ref, tile_ref, out_ref):
    base = pos_ref[0] * 64 + pos_ref[2] * 8
    for dest in range(8):
        col = pl.multiple_of(find(idx_ref, base, dest) * BLK, BLK)
        out_ref[dest] = tile_ref[:, pl.ds(col, BLK)]


def pack_tiles(idx, pos, child):
    def pick_row(step, idx_ref, pos_ref):
        return (find(idx_ref, pos_ref[0] * 64 + pos_ref[1] * 8, step), 0)

    return pl.pallas_call(
        pack_kernel,
        out_shape=jax.ShapeDtypeStruct((64, BLK, BLK), F32),
        grid_spec=pltpu.PrefetchScalarGridSpec(
            num_scalar_prefetch=2,
            grid=(8,),
            in_specs=[pl.BlockSpec((BLK, 8 * BLK), pick_row)],
            out_specs=pl.BlockSpec((8, BLK, BLK), lambda step, idx_ref, pos_ref: (step, 0, 0)),
        ),
        compiler_params=params(),
        name="pack_tiles",
    )(idx, pos, child)


def row_hit(idx_ref, child_id, group, residue):
    base = child_id * 64 + group * 8
    return idx_ref[base + find(idx_ref, base, residue)]


def pick_group(idx_ref, child_id, residue, wanted):
    group = jnp.int32(0)
    found = jnp.int32(0)
    for g in range(8):
        hit = row_hit(idx_ref, child_id, g, residue) == wanted
        group = group + jnp.where(hit, g, 0)
        found = found + jnp.where(hit, 1, 0)
    return group, found


def strip_kernel(idx_ref, pos_ref, parent_ref, tile_ref, out_ref):
    half, res, front = pos_ref[0], pos_ref[1], pos_ref[2]
    owns = (half == 0) & (res < NPB)
    for j in range(16):
        out_ref[j, 0] = jnp.where(owns, parent_ref[:, j * BLK:(j + 1) * BLK], 0.0)
    _, found = pick_group(idx_ref, half, res, res)

    @pl.when((found > 0) & (res < NPB))
    def _():
        for source in range(8):
            col = row_hit(idx_ref, half, source, front) // 8
            out_ref[col, 0] = out_ref[col, 0] + tile_ref[source]

    lead = out_ref[0, 0]
    for j in range(16):
        out_ref[j, 1] = lead


def make_strip(idx, pos, parent, arrived):
    def pick_tiles(step, idx_ref, pos_ref):
        return (pick_group(idx_ref, pos_ref[0], pos_ref[1], pos_ref[1])[0], 0, 0)

    return pl.pallas_call(
        strip_kernel,
        out_shape=jax.ShapeDtypeStruct((16, 2, BLK, BLK), F32),
        grid_spec=pltpu.PrefetchScalarGridSpec(
            num_scalar_prefetch=2,
            grid=(1,),
            in_specs=[
                pl.BlockSpec((BLK, 16 * BLK), lambda step, idx_ref, pos_ref: (0, 0)),
                pl.BlockSpec((8, BLK, BLK), pick_tiles),
            ],
            out_specs=pl.BlockSpec((16, 2, BLK, BLK), lambda step, idx_ref, pos_ref: (0, 0, 0, 0)),
        ),
        compiler_params=params(),
        name="make_strip",
    )(idx, pos, parent, arrived)


def spread_row(tile, j):
    return jnp.broadcast_to(tile[j:j + 1, :], (SUB, BLK))


def spread_col(tile, j):
    return jnp.broadcast_to(tile[:, j:j + 1], (SUB, BLK))


def invert_block(d_ref, b_ref):
    count = BLK // SUB
    row_id = lax.broadcasted_iota(jnp.int32, (SUB, BLK), 0)
    col_id = lax.broadcasted_iota(jnp.int32, (SUB, BLK), 1)
    for t in range(count):
        b_ref[t * SUB:(t + 1) * SUB, :] = jnp.where(col_id == row_id + t * SUB, 1.0, 0.0)
    for t in range(count):
        lead = d_ref[t * SUB:(t + 1) * SUB, :]
        side = b_ref[t * SUB:(t + 1) * SUB, :]
        cols = [spread_col(lead, t * SUB + j) for j in range(SUB)]
        entry = [[spread_row(cols[j], i) if i >= j else None for j in range(SUB)] for i in range(SUB)]
        factor = [[None] * SUB for _ in range(SUB)]
        inv = []
        for k in range(SUB):
            inv.append(1.0 / entry[k][k])
            for i in range(k + 1, SUB):
                factor[i][k] = entry[i][k] * inv[k]
            for i in range(k + 1, SUB):
                for j in range(k + 1, i + 1):
                    entry[i][j] = entry[i][j] - factor[i][k] * entry[j][k]
        rows, sides = [], []
        for j in range(SUB):
            row, extra = spread_row(lead, j), spread_row(side, j)
            for k in range(j):
                row = row - factor[j][k] * rows[k]
                extra = extra - factor[j][k] * sides[k]
            rows.append(row)
            sides.append(extra)
        done = sides[0] * (1.0 / jnp.sqrt(entry[0][0]))
        for j in range(1, SUB):
            done = jnp.where(row_id == j, sides[j] * (1.0 / jnp.sqrt(entry[j][j])), done)
        b_ref[t * SUB:(t + 1) * SUB, :] = done
        for u in range(t + 1, count):
            part = d_ref[u * SUB:(u + 1) * SUB, :]
            extra = b_ref[u * SUB:(u + 1) * SUB, :]
            raw = [spread_col(part, t * SUB + k) for k in range(SUB)]
            for k in range(SUB):
                for q in range(k):
                    raw[k] = raw[k] - factor[k][q] * raw[q]
            for k in range(SUB):
                scale = raw[k] * inv[k]
                part = part - scale * rows[k]
                extra = extra - scale * sides[k]
            d_ref[u * SUB:(u + 1) * SUB, :] = part
            b_ref[u * SUB:(u + 1) * SUB, :] = extra


def lead_kernel(pos_ref, own_ref, one_ref, two_ref, three_ref, out_ref, work_ref, d_ref, b_ref):
    chip = pos_ref[2] // 2
    for away, piece in enumerate((own_ref, one_ref, two_ref, three_ref)):
        source = lax.rem(chip + 4 - away, 4)

        @pl.when(source < 3)
        def _():
            for core in range(2):
                lane = pl.multiple_of(source * 2 * BLK + core * BLK, BLK)
                work_ref[:, pl.ds(lane, BLK)] = piece[core]

    work_ref[:, NPIV:] = jnp.zeros((NPIV, NPIV), F32)

    def eliminate(kb, carry):
        top = pl.multiple_of(kb * BLK, BLK)
        d_ref[...] = work_ref[pl.ds(top, BLK), pl.ds(top, BLK)]
        invert_block(d_ref, b_ref)
        inverse = b_ref[...]
        scaled = jnp.dot(inverse, work_ref[pl.ds(top, BLK), :], precision=EXACT)
        work_ref[pl.ds(top, BLK), :] = scaled
        work_ref[pl.ds(top, BLK), pl.ds(pl.multiple_of(NPIV + kb * BLK, BLK), BLK)] = inverse

        def reduce(i, inner):
            at = pl.multiple_of(i * BLK, BLK)
            lower = work_ref[pl.ds(top, BLK), pl.ds(at, BLK)].T
            work_ref[pl.ds(at, BLK), :] = work_ref[pl.ds(at, BLK), :] - jnp.dot(
                lower, work_ref[pl.ds(top, BLK), :], precision=EXACT)
            return inner

        lax.fori_loop(kb + 1, NPB, reduce, 0)
        return carry

    lax.fori_loop(0, NPB, eliminate, 0)
    out_ref[...] = work_ref[:, NPIV:]


def lead_inverse(pos, pieces):
    spec = pl.BlockSpec((2, NPIV, BLK), lambda step, pos_ref: (0, 0, 0))
    return pl.pallas_call(
        lead_kernel,
        out_shape=jax.ShapeDtypeStruct((NPIV, NPIV), F32),
        grid_spec=pltpu.PrefetchScalarGridSpec(
            num_scalar_prefetch=1,
            grid=(1,),
            in_specs=[spec] * 4,
            out_specs=pl.BlockSpec((NPIV, NPIV), lambda step, pos_ref: (0, 0)),
            scratch_shapes=[
                pltpu.VMEM((NPIV, 2 * NPIV), F32),
                pltpu.VMEM((BLK, BLK), F32),
                pltpu.VMEM((BLK, BLK), F32),
            ],
        ),
        compiler_params=params(),
        name="lead_inverse",
    )(pos, *pieces)


def col_panel_kernel(inverse_ref, strip_ref, high_ref, low_ref):
    strip = jnp.concatenate([strip_ref[0], strip_ref[1]], axis=1)
    panel = jnp.dot(inverse_ref[...], strip, precision=EXACT)
    high = panel.astype(jnp.bfloat16)
    high_ref[...] = high
    low_ref[...] = (panel - high.astype(F32)).astype(jnp.bfloat16)


def col_panel(inverse, strips):
    out = jax.ShapeDtypeStruct((NPIV, 16 * BLK), jnp.bfloat16)
    spec = pl.BlockSpec((NPIV, 2 * BLK), lambda step: (0, step))
    return pl.pallas_call(
        col_panel_kernel,
        out_shape=(out, out),
        grid=(8,),
        in_specs=[
            pl.BlockSpec((NPIV, NPIV), lambda step: (0, 0)),
            pl.BlockSpec((2, NPIV, BLK), lambda step: (step, 0, 0)),
        ],
        out_specs=(spec, spec),
        compiler_params=params(),
        name="col_panel",
    )(inverse, strips)


def row_panel_kernel(inverse_ref, strip_ref, out_ref):
    strip = jnp.concatenate([strip_ref[0], strip_ref[1]], axis=1)
    out_ref[...] = jnp.dot(inverse_ref[...], strip, precision=EXACT).T


def row_panel(inverse, strips):
    return pl.pallas_call(
        row_panel_kernel,
        out_shape=jax.ShapeDtypeStruct((8 * BLK, NPIV), F32),
        grid=(4,),
        in_specs=[
            pl.BlockSpec((NPIV, NPIV), lambda step: (0, 0)),
            pl.BlockSpec((2, NPIV, BLK), lambda step: (step, 0, 0)),
        ],
        out_specs=pl.BlockSpec((2 * BLK, NPIV), lambda step: (step, 0)),
        compiler_params=params(),
        name="row_panel",
    )(inverse, strips)


def finish_kernel(idx_ref, pos_ref, parent_ref, own_ref, other_ref, rows_ref, high_ref, low_ref, out_ref):
    half, res, front = pos_ref[0], pos_ref[1], pos_ref[2]
    step = pl.program_id(0)
    row_block = half * 8 + res + 16 * step
    rows = rows_ref[...]
    row_high = rows.astype(jnp.bfloat16)
    row_low = (rows - row_high.astype(F32)).astype(jnp.bfloat16)
    high = high_ref[...]
    product = jnp.dot(row_high, low_ref[...], preferred_element_type=F32)
    product = product + jnp.dot(row_low, high, preferred_element_type=F32)
    product = product + jnp.dot(row_high, high, preferred_element_type=F32)
    out_ref[...] = parent_ref[...] - product
    for child_id, tiles in ((half, own_ref), (1 - half, other_ref)):
        _, found = pick_group(idx_ref, child_id, res, row_block)

        @pl.when(found > 0)
        def _():
            for source in range(8):
                col = row_hit(idx_ref, child_id, source, front) // 8
                at = pl.ds(pl.multiple_of(col * BLK, BLK), BLK)
                out_ref[:, at] = out_ref[:, at] + tiles[source]

    @pl.when(row_block < NPB)
    def _():
        out_ref[...] = jnp.zeros_like(out_ref)

    @pl.when(front < NPB)
    def _():
        panel = rows_ref[:, pl.ds(pl.multiple_of(lax.min(front, NPB - 1) * BLK, BLK), BLK)]
        row_id = lax.broadcasted_iota(jnp.int32, (BLK, BLK), 0) + row_block * BLK
        col_id = lax.broadcasted_iota(jnp.int32, (BLK, BLK), 1) + front * BLK
        out_ref[:, :BLK] = jnp.where(row_id >= col_id, panel, 0.0)


def finish(idx, pos, parent, arrived, crossed, rows, high, low):
    def pick(step, idx_ref, pos_ref, child_id):
        row_block = pos_ref[0] * 8 + pos_ref[1] + 16 * step
        return (pick_group(idx_ref, child_id, pos_ref[1], row_block)[0], 0, 0)

    whole = pl.BlockSpec((NPIV, 16 * BLK), lambda step, idx_ref, pos_ref: (0, 0))
    return pl.pallas_call(
        finish_kernel,
        out_shape=jax.ShapeDtypeStruct((8 * BLK, 16 * BLK), F32),
        grid_spec=pltpu.PrefetchScalarGridSpec(
            num_scalar_prefetch=2,
            grid=(8,),
            in_specs=[
                pl.BlockSpec((BLK, 16 * BLK), lambda step, idx_ref, pos_ref: (step, 0)),
                pl.BlockSpec((8, BLK, BLK), lambda step, idx_ref, pos_ref: pick(step, idx_ref, pos_ref, pos_ref[0])),
                pl.BlockSpec((8, BLK, BLK), lambda step, idx_ref, pos_ref: pick(step, idx_ref, pos_ref, 1 - pos_ref[0])),
                pl.BlockSpec((BLK, NPIV), lambda step, idx_ref, pos_ref: (step, 0)),
                whole,
                whole,
            ],
            out_specs=pl.BlockSpec((BLK, 16 * BLK), lambda step, idx_ref, pos_ref: (step, 0)),
        ),
        compiler_params=params(),
        name="finish",
    )(idx, pos, parent, arrived, crossed, rows, high, low)


def body(parent_front, child_entries, child_index):
    idx = child_index.reshape(-1)
    pos = jnp.stack([lax.axis_index("half"), lax.axis_index("res"), lax.axis_index("front")]).astype(jnp.int32)
    packed = pack_tiles(idx, pos, child_entries)
    arrived = lax.all_to_all(packed, ("res", "front"), split_axis=0, concat_axis=0, tiled=True)

    strip = make_strip(idx, pos, parent_front, arrived)
    pieces = lax.all_to_all(strip, CUBE, split_axis=0, concat_axis=0, tiled=True)
    summed = pieces[:NPB] + pieces[8:8 + NPB]
    one_block = summed[:, 0].reshape(NPIV, BLK)
    lead_cols = summed[:, 1].reshape(NPIV, BLK)

    beside = lax.ppermute(lead_cols, "front", [(i, i ^ 1) for i in range(8)])
    odd = lax.axis_index("front") % 2 == 1
    pair = jnp.stack([jnp.where(odd, beside, lead_cols), jnp.where(odd, lead_cols, beside)])
    pair_parts = [pair]
    for away in range(1, 4):
        hops = [(i, (i + 2 * away) % 8) for i in range(6)]
        pair_parts.append(lax.ppermute(pair, "front", hops))

    strips = lax.all_gather(one_block, CUBE, axis=0, tiled=False)
    moved = lax.ppermute(one_block, ("half", "res", "front"),
                         [(c + 16 * f, c * 8 + f) for c in range(16) for f in range(8)])
    row_strips = lax.all_gather(moved, "front", axis=0, tiled=False)
    crossed = lax.ppermute(arrived, "half", [(0, 1), (1, 0)])

    inverse = lead_inverse(pos, pair_parts)
    high, low = col_panel(inverse, strips)
    rows = row_panel(inverse, row_strips)
    return finish(idx, pos, parent_front, arrived, crossed, rows, high, low)


def solution(mesh):
    split = Mesh(mesh.devices.reshape(2, 8, 8), ("half", "res", "front"))
    placed = P(CUBE, "front")
    return jax.shard_map(
        body, mesh=split, in_specs=(placed, placed, P()), out_specs=placed, check_vma=False
    )
```

time: 1980 us -> 331 us (0.17)
  waiting for transfers between devices: 1460 us -> 60.7 us
  other arithmetic: 188 us -> 0.85 us
  local copies, waits for them, and re-layouts: 164 us -> 3.05 us
  matrix products: 131 us -> 0 us
  Pallas kernels: 0 us -> 124 us
  blocking collectives: 0 us -> 95.5 us
  starting transfers between devices: 12.3 us -> 32.6 us
    psum x18 -> x0, waiting for transfers between devices: 1370 us -> none  [spread_2(): return lax.psum(block, axis)]
    another operation x38 -> x3, other arithmetic: 145 us -> 0.76 us  [the longest x1 0.65 us: body(): jnp.stack([lax.axis_index('half'), lax.axis_index('res'), lax.axis_index(...]
    dot_general x17 -> x0, matrix products: 129 us -> none  [the longest x6 72.8 us: apply_step(): jnp.dot(row_panel, panel_part.T, precision=EXACT)]
    pallas_call x0 -> x6, Pallas kernels: none -> 124 us  [the longest x1 51.7 us: lead_inverse(): pl.pallas_call(lead_kernel, out_shape=jax.ShapeDtypeStruct((NPIV, NPIV),...]
    all_to_all x0 -> x2, blocking collectives: none -> 95.5 us  [the longest x1 61.1 us: body(): lax.all_to_all(packed, ('res', 'front'), split_axis=0, concat_axis=0, til...]
    all_to_all x1 -> x0, waiting for transfers between devices: 88.6 us -> none  [body(): lax.all_to_all(flat_tiles, ('cube', 'front'), split_axis=0, concat_axis=0...]
    while x19 -> x0, local copies, waits for them, and re-layouts: 63.9 us -> none
    ppermute x0 -> x6, waiting for transfers between devices: none -> 44.7 us  [the longest x3 43 us: body(): pair_parts.append(lax.ppermute(pair, 'front', hops))]
  transfers between devices with their start and end apart: 19 -> 8, of which waited for: 19 -> 5; matrix products, arithmetic and copies ran while one was open for 1% -> 0% of each run, Pallas kernels for 0% -> 25%
where the time goes in v1:
time: 331 us; the launch traced here: 330 us
  Pallas kernels  124 us (37%)
  blocking collectives  95.5 us (29%)
  waiting for transfers between devices  60.7 us (18%)
  starting transfers between devices  32.6 us (10%)
  between operations  13.5 us (4%)
    all_to_all x1, blocking collectives, body(): lax.all_to_all(packed, ('res', 'front'), split_axis=0, concat_axis=0, til...  61.1 us
    pallas_call x1, Pallas kernels, lead_inverse(): pl.pallas_call(lead_kernel, out_shape=jax.ShapeDtypeStruct((NPIV, NPIV),...  51.7 us
    ppermute x3, waiting for transfers between devices, body(): pair_parts.append(lax.ppermute(pair, 'front', hops))  43 us
    all_to_all x1, blocking collectives, body(): lax.all_to_all(strip, CUBE, split_axis=0, concat_axis=0, tiled=True)  34.4 us
    pallas_call x1, Pallas kernels, finish(): pl.pallas_call(finish_kernel, out_shape=jax.ShapeDtypeStruct((8 * BLK, 16...  29.7 us
    ppermute x1, starting transfers between devices, body(): crossed = lax.ppermute(arrived, 'half', [(0, 1), (1, 0)])  24.3 us
    pallas_call x1, Pallas kernels, col_panel(): pl.pallas_call(col_panel_kernel, out_shape=(out, out), grid=(8,), in_spec...  19.6 us
    all_gather x1, waiting for transfers between devices, body(): strips = lax.all_gather(one_block, CUBE, axis=0, tiled=False)  15.3 us
  transfers between devices with their start and end apart: 8, of which 5 were waited for; matrix products, arithmetic and copies ran while one was open for 0% of the time, Pallas kernels for 25%

profile of v1, /device:TPU:0, one launch (start us, length us, event | category | flops | bytes accessed | tf_op | source)
XLA Modules:
  0.0 330.2 jit_solution(16501767534972851257)
XLA Ops:
  6.5 1.3 reshape.3.idx_ref
  7.9 0.7 pad_add_fusion.pos_ref
  8.5 7.7 %pack_tiles.1 = f32[64,128,128]{2,1,0:T(8,128)} custom-call(s32[128]{0:T(128)} %reshape.3.idx_ref, s32[3]{0:T(128)} %pad_add_fusion.pos_ref, f32[1024,1024]{1,0:T(8,128)} %tile_ref.1), custom_call_target="tpu_custom_call" | custom-call | tf_op jit(solution)/shard_map/pack_tiles/pallas_call | solution.py:43
  16.2 61.1 %all_to_all.10.tile_ref.own_ref = f32[64,128,128]{2,1,0:T(8,128)} all-to-all(f32[64,128,128]{2,1,0:T(8,128)} %pack_tiles.1), channel_id=1, replica_groups=mesh['half'=2,'res'=8,'front'=8] {'res','front'}, dimensions={0} | all-to-all | bytes 8388608 | tf_op jit(solution)/shard_map/all_to_all | solution.py:333
  77.3 3.9 %make_strip.1 = f32[16,2,128,128]{3,2,1,0:T(8,128)} custom-call(s32[128]{0:T(128)} %reshape.3.idx_ref, s32[3]{0:T(128)} %pad_add_fusion.pos_ref, f32[1024,2048]{1,0:T(8,128)} %parent_ref.3, f32[64,128,128]{2,1,0:T(8,128)} %all_to_all.10.tile_ref.own_ref), custom_call_target="tpu_custom_call" | custom-call | tf_op jit(solution)/shard_map/make_strip/pallas_call | solution.py:94
  81.2 34.4 %all_to_all.11 = f32[16,2,128,128]{3,2,1,0:T(8,128)S(1)} all-to-all(f32[16,2,128,128]{3,2,1,0:T(8,128)} %make_strip.1), channel_id=1, replica_groups=mesh['half'=2,'res'=8,'front'=8] {'half','res'}, dimensions={0} | all-to-all | bytes 4194304 | tf_op jit(solution)/shard_map/all_to_all | solution.py:336
  115.6 0.1 slice_add_fusion
  115.8 0.7 collective-permute-start.5
  116.5 0.8 copy-done.5
  117.3 0.7 all-gather.4.cloned.1.call-update
  118.0 24.3 %collective-permute-start = (f32[64,128,128]{2,1,0:T(8,128)}, f32[64,128,128]{2,1,0:T(8,128)}, u32[]{:S(2)}, u32[]{:S(2)}) collective-permute-start(f32[64,128,128]{2,1,0:T(8,128)} %all_to_all.10.tile_ref.own_ref), channel_id=1, source_target_pairs={{0,64},{64,0},{1,65},{65,1},{2,66},{66,2},{3,67},{67,3},{4,68},{68... | collective-permute-start | bytes 12582920 | tf_op jit(solution)/shard_map/ppermute | solution.py:353
  142.3 1.7 collective-permute-done.1
  144.2 3.4 %collective-permute-start.4 = (f32[2,768,128]{2,1,0:T(8,128)S(1)}, f32[2,768,128]{2,1,0:T(8,128)S(1)}, u32[]{:S(2)}, u32[]{:S(2)}) collective-permute-start(f32[2,768,128]{2,1,0:T(8,128)S(1)} %pad_maximum_fusion.own_ref), channel_id=1, source_target_pairs={{0,6},{1,7},{2,0},{3,1},{4,2},{5,3},{8,14},{9,15},{10,8},{11,9},{1... | collective-permute-start | bytes 2359304 | tf_op jit(solution)/shard_map/ppermute | solution.py:347
  147.6 1.9 collective-permute-start.3
  149.5 2.2 collective-permute-start.2
  151.7 27.4 %collective-permute-done.4.three_ref = f32[2,768,128]{2,1,0:T(8,128)S(1)} collective-permute-done((f32[2,768,128]{2,1,0:T(8,128)S(1)}, f32[2,768,128]{2,1,0:T(8,128)S(1)}, u32[]{:S(2)}, u32[]{:S(2)}) %collective-permute-start.4) | collective-permute-done | bytes 786464 | tf_op jit(solution)/shard_map/ppermute | solution.py:347
  179.1 1.7 collective-permute-done.3.two_ref
  180.9 13.9 %collective-permute-done.2.one_ref = f32[2,768,128]{2,1,0:T(8,128)S(1)} collective-permute-done((f32[2,768,128]{2,1,0:T(8,128)S(1)}, f32[2,768,128]{2,1,0:T(8,128)S(1)}, u32[]{:S(2)}, u32[]{:S(2)}) %collective-permute-start.2) | collective-permute-done | bytes 786464 | tf_op jit(solution)/shard_map/ppermute | solution.py:347
  194.8 0.9 copy-done.4
  195.7 51.7 %lead_inverse.1.inverse_ref = f32[768,768]{1,0:T(8,128)} custom-call(s32[3]{0:T(128)} %pad_add_fusion.pos_ref, f32[2,768,128]{2,1,0:T(8,128)} %copy-done, f32[2,768,128]{2,1,0:T(8,128)} %copy-done.4, f32[2,768,128]{2,1,0:T(8,128)} %copy-done.3, f32[2,768,128]{2,1,0:T(8,128)} %copy-done.2), custom_call_target="tpu_custom_call" | custom-call | tf_op jit(solution)/shard_map/lead_inverse/pallas_call | solution.py:204
  247.4 11.4 %row_panel.1.rows_ref = f32[1024,768]{1,0:T(8,128)} custom-call(f32[768,768]{1,0:T(8,128)} %lead_inverse.1.inverse_ref, f32[8,768,128]{2,1,0:T(8,128)} %bitcast.13), custom_call_target="tpu_custom_call" | custom-call | tf_op jit(solution)/shard_map/row_panel/pallas_call | solution.py:254
  258.8 15.3 %all-gather.4.cloned.1.call-done.strip_ref = f32[16,768,128]{2,1,0:T(8,128)} async-done(((f32[1,768,128]{2,1,0:T(8,128)}), f32[16,768,128]{2,1,0:T(8,128)}) %all-gather.4.cloned.1.call-update) | async-done | bytes 6291472 | tf_op jit(solution)/shard_map/all_gather | solution.py:349
  274.1 19.6 %col_panel.1 = (bf16[768,2048]{1,0:T(8,128)(2,1)}, bf16[768,2048]{1,0:T(8,128)(2,1)}) custom-call(f32[768,768]{1,0:T(8,128)} %lead_inverse.1.inverse_ref, f32[16,768,128]{2,1,0:T(8,128)} %all-gather.4.cloned.1.call-done.strip_ref), custom_call_target="tpu_custom_call" | custom-call | tf_op jit(solution)/shard_map/col_panel/pallas_call | solution.py:234
  293.7 29.7 %finish.1 = f32[1024,2048]{1,0:T(8,128)} custom-call(s32[128]{0:T(128)} %reshape.3.idx_ref, s32[3]{0:T(128)} %pad_add_fusion.pos_ref, f32[1024,2048]{1,0:T(8,128)} %parent_ref.3, f32[64,128,128]{2,1,0:T(8,128)} %all_to_all.10.tile_ref.own_ref, f32[64,128,128]{2,1,0:T(8,128)} %collective-permute-done.other_ref, f32[1024,768]{1,0:T(8,128)} %row_panel.1.rows_ref, ...), custom_call_target="tpu_custom_call" | custom-call | tf_op jit(solution)/shard_map/finish/pallas_call | solution.py:308
  (20 shorter events, 0.2 us)
Async XLA Ops:
  6.5 240.8 %all-gather.6.cloned.1.call-start = ((), (), s32[]{:S(2)}) async-start(), calls=%async_computation.3 | async-start | bytes 3538944 | tf_op jit(solution)/shard_map/all_gather | solution.py:352
  115.8 1.6 copy-start.1
  115.8 0.7 collective-permute-start.5
  116.5 0.8 copy-start.5
  117.3 156.8 %all-gather.4.cloned.1.call-start = ((), (), s32[]{:S(2)}) async-start(), calls=%async_computation.2 | async-start | bytes 6684672 | tf_op jit(solution)/shard_map/all_gather | solution.py:349
  118.0 175.7 %collective-permute-start = (f32[64,128,128]{2,1,0:T(8,128)}, f32[64,128,128]{2,1,0:T(8,128)}, u32[]{:S(2)}, u32[]{:S(2)}) collective-permute-start(f32[64,128,128]{2,1,0:T(8,128)} %all_to_all.10.tile_ref.own_ref), channel_id=1, source_target_pairs={{0,64},{64,0},{1,65},{65,1},{2,66},{66,2},{3,67},{67,3},{4,68},{68... | collective-permute-start | bytes 12582920 | tf_op jit(solution)/shard_map/ppermute | solution.py:353
  142.3 1.7 collective-permute-start.1
  144.2 50.6 %copy-start = (f32[2,768,128]{2,1,0:T(8,128)}, f32[2,768,128]{2,1,0:T(8,128)S(1)}, u32[]{:S(2)}) copy-start(f32[2,768,128]{2,1,0:T(8,128)S(1)} %pad_maximum_fusion.own_ref) | copy-start | bytes 2359300
  144.2 34.9 %collective-permute-start.4 = (f32[2,768,128]{2,1,0:T(8,128)S(1)}, f32[2,768,128]{2,1,0:T(8,128)S(1)}, u32[]{:S(2)}, u32[]{:S(2)}) collective-permute-start(f32[2,768,128]{2,1,0:T(8,128)S(1)} %pad_maximum_fusion.own_ref), channel_id=1, source_target_pairs={{0,6},{1,7},{2,0},{3,1},{4,2},{5,3},{8,14},{9,15},{10,8},{11,9},{1... | collective-permute-start | bytes 2359304 | tf_op jit(solution)/shard_map/ppermute | solution.py:347
  147.6 33.3 %collective-permute-start.3 = (f32[2,768,128]{2,1,0:T(8,128)S(1)}, f32[2,768,128]{2,1,0:T(8,128)S(1)}, u32[]{:S(2)}, u32[]{:S(2)}) collective-permute-start(f32[2,768,128]{2,1,0:T(8,128)S(1)} %pad_maximum_fusion.own_ref), channel_id=1, source_target_pairs={{0,4},{1,5},{2,6},{3,7},{4,0},{5,1},{8,12},{9,13},{10,14},{11,15},... | collective-permute-start | bytes 2359304 | tf_op jit(solution)/shard_map/ppermute | solution.py:347
  149.5 45.2 %collective-permute-start.2 = (f32[2,768,128]{2,1,0:T(8,128)S(1)}, f32[2,768,128]{2,1,0:T(8,128)S(1)}, u32[]{:S(2)}, u32[]{:S(2)}) collective-permute-start(f32[2,768,128]{2,1,0:T(8,128)S(1)} %pad_maximum_fusion.own_ref), channel_id=1, source_target_pairs={{0,2},{1,3},{2,4},{3,5},{4,6},{5,7},{8,10},{9,11},{10,12},{11,13},... | collective-permute-start | bytes 2359304 | tf_op jit(solution)/shard_map/ppermute | solution.py:347
  179.1 15.6 %copy-start.2 = (f32[2,768,128]{2,1,0:T(8,128)}, f32[2,768,128]{2,1,0:T(8,128)S(1)}, u32[]{:S(2)}) copy-start(f32[2,768,128]{2,1,0:T(8,128)S(1)} %collective-permute-done.4.three_ref) | copy-start | bytes 2359300
  180.9 13.9 %copy-start.3 = (f32[2,768,128]{2,1,0:T(8,128)}, f32[2,768,128]{2,1,0:T(8,128)S(1)}, u32[]{:S(2)}) copy-start(f32[2,768,128]{2,1,0:T(8,128)S(1)} %collective-permute-done.3.two_ref) | copy-start | bytes 2359300
  194.8 0.9 copy-start.4
Sparse Core Ops, SparseCore 0:
  117.4 65.4 all-gather.5
  185.0 89.0 all-gather.3

commit v2 on v1

v2 whole, which is shorter than its diff:
```python
import jax
import jax.numpy as jnp
from jax import lax
from jax.experimental import pallas as pl
from jax.experimental.pallas import tpu as pltpu
from jax.sharding import Mesh, PartitionSpec as P


BLK = 128
NPB = 6
NPIV = NPB * BLK
SUB = 8

EXACT = lax.Precision.HIGHEST
F32 = jnp.float32
CUBE = ("zh", "zl", "y")
FRONT = ("x", "core")
VMEM_LIMIT = 56 * 1024 * 1024


GROUP = 0
COLUMN = 16
ROW_PICK = 32
COL_PICK = 40
PIVOT = 48
HALF, RES, FRONT_AT = 50, 51, 52
SPARE = 53
TABLE = 64


def params():
    return pltpu.CompilerParams(vmem_limit_bytes=VMEM_LIMIT)


def table_kernel(pos_ref, idx_ref, tab_ref):
    half, res, front = pos_ref[0], pos_ref[1], pos_ref[2]
    for at in range(TABLE):
        tab_ref[at] = jnp.int32(-1)
    tab_ref[HALF], tab_ref[RES], tab_ref[FRONT_AT] = half, res, front
    for child_id in range(2):
        for run in range(8):
            row, col = jnp.int32(0), jnp.int32(0)
            for u in range(8):
                entry = idx_ref[child_id, run * 8 + u]
                residue = entry & 7
                row = jnp.where(residue == res, entry, row)
                col = jnp.where(residue == front, entry, col)
            mine = ((row >> 3) & 1) == half
            tab_ref[jnp.where(mine, GROUP + child_id * 8 + (row >> 4), SPARE)] = jnp.int32(run)
            tab_ref[jnp.where(row == res, PIVOT + child_id, SPARE)] = jnp.int32(run)
            tab_ref[COLUMN + child_id * 8 + run] = col >> 3
    for u in range(8):
        tab_ref[ROW_PICK + (idx_ref[half, res * 8 + u] & 7)] = jnp.int32(u)
        tab_ref[COL_PICK + (idx_ref[half, front * 8 + u] & 7)] = jnp.int32(u)


def make_table(pos, idx):
    smem = pl.BlockSpec(memory_space=pltpu.SMEM)
    return pl.pallas_call(
        table_kernel,
        out_shape=jax.ShapeDtypeStruct((TABLE,), jnp.int32),
        in_specs=[smem, smem],
        out_specs=smem,
        name="make_table",
    )(pos, idx)


def pack_kernel(tab_ref, tile_ref, out_ref):
    for dest in range(8):
        col = pl.multiple_of(tab_ref[COL_PICK + dest] * BLK, BLK)
        out_ref[dest] = tile_ref[:, pl.ds(col, BLK)]


def pack_tiles(tab, child):
    return pl.pallas_call(
        pack_kernel,
        out_shape=jax.ShapeDtypeStruct((64, BLK, BLK), F32),
        grid_spec=pltpu.PrefetchScalarGridSpec(
            num_scalar_prefetch=1,
            grid=(8,),
            in_specs=[pl.BlockSpec((BLK, 8 * BLK), lambda step, tab_ref: (tab_ref[ROW_PICK + step], 0))],
            out_specs=pl.BlockSpec((8, BLK, BLK), lambda step, tab_ref: (step, 0, 0)),
        ),
        compiler_params=params(),
        name="pack_tiles",
    )(tab, child)


def strip_kernel(tab_ref, parent_ref, tile_ref, out_ref):
    half, res = tab_ref[HALF], tab_ref[RES]
    owns = (half == 0) & (res < NPB)

    @pl.when(owns)
    def _():
        for j in range(16):
            out_ref[j, 0] = parent_ref[:, j * BLK:(j + 1) * BLK]

    @pl.when(jnp.logical_not(owns))
    def _():
        for j in range(16):
            out_ref[j, 0] = jnp.zeros((BLK, BLK), F32)

    @pl.when((tab_ref[PIVOT + half] >= 0) & (res < NPB))
    def _():
        for source in range(8):
            col = tab_ref[COLUMN + half * 8 + source]
            out_ref[col, 0] = out_ref[col, 0] + tile_ref[source]

    lead = out_ref[0, 0]
    for j in range(16):
        out_ref[j, 1] = lead


def make_strip(tab, parent, arrived):
    def pick_tiles(step, tab_ref):
        return (lax.max(tab_ref[PIVOT + tab_ref[HALF]], 0), 0, 0)

    return pl.pallas_call(
        strip_kernel,
        out_shape=jax.ShapeDtypeStruct((16, 2, BLK, BLK), F32),
        grid_spec=pltpu.PrefetchScalarGridSpec(
            num_scalar_prefetch=1,
            grid=(1,),
            in_specs=[
                pl.BlockSpec((BLK, 16 * BLK), lambda step, tab_ref: (0, 0)),
                pl.BlockSpec((8, BLK, BLK), pick_tiles),
            ],
            out_specs=pl.BlockSpec((16, 2, BLK, BLK), lambda step, tab_ref: (0, 0, 0, 0)),
        ),
        compiler_params=params(),
        name="make_strip",
    )(tab, parent, arrived)


def spread_row(tile, j):
    return jnp.broadcast_to(tile[j:j + 1, :], (SUB, BLK))


def spread_col(tile, j):
    return jnp.broadcast_to(tile[:, j:j + 1], (SUB, BLK))


def invert_block(d_ref, b_ref):
    count = BLK // SUB
    row_id = lax.broadcasted_iota(jnp.int32, (SUB, BLK), 0)
    col_id = lax.broadcasted_iota(jnp.int32, (SUB, BLK), 1)
    for t in range(count):
        b_ref[t * SUB:(t + 1) * SUB, :] = jnp.where(col_id == row_id + t * SUB, 1.0, 0.0)
    for t in range(count):
        lead = d_ref[t * SUB:(t + 1) * SUB, :]
        side = b_ref[t * SUB:(t + 1) * SUB, :]
        cols = [spread_col(lead, t * SUB + j) for j in range(SUB)]
        entry = [[spread_row(cols[j], i) if i >= j else None for j in range(SUB)] for i in range(SUB)]
        factor = [[None] * SUB for _ in range(SUB)]
        inv = []
        for k in range(SUB):
            inv.append(1.0 / entry[k][k])
            for i in range(k + 1, SUB):
                factor[i][k] = entry[i][k] * inv[k]
            for i in range(k + 1, SUB):
                for j in range(k + 1, i + 1):
                    entry[i][j] = entry[i][j] - factor[i][k] * entry[j][k]
        rows, sides = [], []
        for j in range(SUB):
            row, extra = spread_row(lead, j), spread_row(side, j)
            for k in range(j):
                row = row - factor[j][k] * rows[k]
                extra = extra - factor[j][k] * sides[k]
            rows.append(row)
            sides.append(extra)
        done = sides[0] * (1.0 / jnp.sqrt(entry[0][0]))
        for j in range(1, SUB):
            done = jnp.where(row_id == j, sides[j] * (1.0 / jnp.sqrt(entry[j][j])), done)
        b_ref[t * SUB:(t + 1) * SUB, :] = done
        for u in range(t + 1, count):
            part = d_ref[u * SUB:(u + 1) * SUB, :]
            extra = b_ref[u * SUB:(u + 1) * SUB, :]
            raw = [spread_col(part, t * SUB + k) for k in range(SUB)]
            for k in range(SUB):
                for q in range(k):
                    raw[k] = raw[k] - factor[k][q] * raw[q]
            for k in range(SUB):
                scale = raw[k] * inv[k]
                part = part - scale * rows[k]
                extra = extra - scale * sides[k]
            d_ref[u * SUB:(u + 1) * SUB, :] = part
            b_ref[u * SUB:(u + 1) * SUB, :] = extra


def lead_kernel(tab_ref, *refs):
    pieces, (out_ref, work_ref, d_ref, b_ref) = refs[:8], refs[8:]
    chip, core = tab_ref[FRONT_AT] // 2, lax.rem(tab_ref[FRONT_AT], 2)
    for away in range(4):
        source = lax.rem(chip + 4 - away, 4)

        @pl.when(source < 3)
        def _():
            for other in range(2):
                lane = (source * 2 + lax.rem(core + other, 2)) * BLK
                work_ref[:, pl.ds(pl.multiple_of(lane, BLK), BLK)] = pieces[4 * other + away][...]

    for i in range(NPB):
        rows = slice(i * BLK, (i + 1) * BLK)
        row_id = lax.broadcasted_iota(jnp.int32, (BLK, NPIV), 0) + i * BLK
        col_id = lax.broadcasted_iota(jnp.int32, (BLK, NPIV), 1)
        work_ref[rows, NPIV:] = jnp.where(row_id == col_id, 1.0, 0.0)

    def eliminate(kb, carry):
        top = pl.ds(pl.multiple_of(kb * BLK, BLK), BLK)
        window = pl.ds(pl.multiple_of((kb + 1) * BLK, BLK), NPIV)
        d_ref[...] = work_ref[top, top]
        invert_block(d_ref, b_ref)
        work_ref[top, window] = jnp.dot(b_ref[...], work_ref[top, window], precision=EXACT)
        for k in range(NPB - 1):

            @pl.when(kb == k)
            def _():
                pivot = slice(k * BLK, (k + 1) * BLK)
                below = slice((k + 1) * BLK, NPIV)
                wide = slice((k + 1) * BLK, (k + 1) * BLK + NPIV)
                lower = work_ref[pivot, below].T
                work_ref[below, wide] = work_ref[below, wide] - jnp.dot(
                    lower, work_ref[pivot, wide], precision=EXACT)

        return carry

    lax.fori_loop(0, NPB, eliminate, 0)
    out_ref[...] = work_ref[:, NPIV:]


def lead_inverse(tab, pieces):
    return pl.pallas_call(
        lead_kernel,
        out_shape=jax.ShapeDtypeStruct((NPIV, NPIV), F32),
        grid_spec=pltpu.PrefetchScalarGridSpec(
            num_scalar_prefetch=1,
            grid=(1,),
            in_specs=[pl.BlockSpec((NPIV, BLK), lambda step, tab_ref: (0, 0))] * 8,
            out_specs=pl.BlockSpec((NPIV, NPIV), lambda step, tab_ref: (0, 0)),
            scratch_shapes=[
                pltpu.VMEM((NPIV, 2 * NPIV), F32),
                pltpu.VMEM((BLK, BLK), F32),
                pltpu.VMEM((BLK, BLK), F32),
            ],
        ),
        compiler_params=params(),
        name="lead_inverse",
    )(tab, *pieces)


def halves(value):
    high = value.astype(jnp.bfloat16)
    return high, (value - high.astype(F32)).astype(jnp.bfloat16)


def dot_halves(left, right):
    product = jnp.dot(left[0], right[1], preferred_element_type=F32)
    product = product + jnp.dot(left[1], right[0], preferred_element_type=F32)
    return product + jnp.dot(left[0], right[0], preferred_element_type=F32)


def whole(*shape):
    return pl.BlockSpec(shape, lambda step, tab_ref: (0,) * len(shape))


def col_kernel(inverse_ref, strip_ref, out_ref):
    inverse = halves(inverse_ref[...])
    strip = jnp.concatenate([strip_ref[0], strip_ref[1], strip_ref[2], strip_ref[3]], axis=1)
    high, low = halves(dot_halves(inverse, halves(strip)))
    out_ref[:NPIV, :] = low
    out_ref[NPIV:, :] = high


def col_panel(inverse, piece):
    return pl.pallas_call(
        col_kernel,
        out_shape=jax.ShapeDtypeStruct((2 * NPIV, 4 * BLK), jnp.bfloat16),
        compiler_params=params(),
        name="col_panel",
    )(inverse, piece)


def row_kernel(tab_ref, inverse_ref, *refs):
    row_refs, rows_ref = refs[:8], refs[8]
    chip, core = tab_ref[FRONT_AT] // 2, lax.rem(tab_ref[FRONT_AT], 2)
    inverse = halves(inverse_ref[...])
    for away in range(4):
        strip = jnp.concatenate([row_refs[away][...], row_refs[4 + away][...]], axis=1)
        panel = dot_halves(inverse, halves(strip)).T
        pair = lax.rem(chip + 8 - away - tab_ref[RES] // 2, 4)
        for other in range(2):
            at = (pair * 2 + lax.rem(core + other, 2)) * BLK
            rows_ref[pl.ds(pl.multiple_of(at, BLK), BLK), :] = panel[other * BLK:(other + 1) * BLK]


def row_panel(tab, inverse, pieces):
    return pl.pallas_call(
        row_kernel,
        out_shape=jax.ShapeDtypeStruct((8 * BLK, NPIV), F32),
        grid_spec=pltpu.PrefetchScalarGridSpec(
            num_scalar_prefetch=1,
            grid=(1,),
            in_specs=[whole(NPIV, NPIV)] + [whole(NPIV, BLK)] * 8,
            out_specs=whole(8 * BLK, NPIV),
        ),
        compiler_params=params(),
        name="row_panel",
    )(tab, inverse, *pieces)


def slot_col(tab_ref, slot):
    z = tab_ref[HALF] * 2 + tab_ref[RES] // 4
    y = lax.rem(tab_ref[RES], 4)
    return lax.rem(z + 4 - slot % 4, 4) * 4 + lax.rem(y + 4 - slot // 4, 4)


def finish_kernel(tab_ref, parent_ref, own0, own1, other0, other1, rows_ref, *refs):
    col_refs, out_ref = refs[:4], refs[4]
    half, res, front = tab_ref[HALF], tab_ref[RES], tab_ref[FRONT_AT]
    step = pl.program_id(0)
    high, low = halves(rows_ref[...])
    both = jnp.concatenate([high, low], axis=1)
    for away in range(4):
        product = jnp.dot(both, col_refs[away][...], preferred_element_type=F32)
        product = product + jnp.dot(high, col_refs[away][NPIV:, :], preferred_element_type=F32)
        for part in range(4):
            at = pl.ds(pl.multiple_of(slot_col(tab_ref, 4 * away + part) * BLK, BLK), BLK)
            out_ref[:, at] = parent_ref[:, at] - product[:, part * BLK:(part + 1) * BLK]
    for part, tile_refs in enumerate(((own0, other0), (own1, other1))):
        row_block = half * 8 + res + 16 * (2 * step + part)
        rows = slice(part * BLK, (part + 1) * BLK)
        for child_id, tiles in ((half, tile_refs[0]), (1 - half, tile_refs[1])):
            group = tab_ref[GROUP + child_id * 8 + 2 * step + part]

            @pl.when(group >= 0)
            def _():
                for source in range(8):
                    col = tab_ref[COLUMN + child_id * 8 + source]
                    at = pl.ds(pl.multiple_of(col * BLK, BLK), BLK)
                    out_ref[rows, at] = out_ref[rows, at] + tiles[source]

        @pl.when(row_block < NPB)
        def _():
            out_ref[rows, :] = jnp.zeros((BLK, 16 * BLK), F32)

        @pl.when(front < NPB)
        def _():
            lane = pl.multiple_of(lax.min(front, NPB - 1) * BLK, BLK)
            row_id = lax.broadcasted_iota(jnp.int32, (BLK, BLK), 0) + row_block * BLK
            col_id = lax.broadcasted_iota(jnp.int32, (BLK, BLK), 1) + front * BLK
            out_ref[rows, :BLK] = jnp.where(row_id >= col_id, rows_ref[rows, pl.ds(lane, BLK)], 0.0)


def finish(tab, parent, arrived, crossed, rows, cols):
    def tiles(own, part):
        def pick(step, tab_ref):
            child_id = tab_ref[HALF] if own else 1 - tab_ref[HALF]
            return (lax.max(tab_ref[GROUP + child_id * 8 + 2 * step + part], 0), 0, 0)

        return pl.BlockSpec((8, BLK, BLK), pick)

    wide = pl.BlockSpec((2 * NPIV, 4 * BLK), lambda step, tab_ref: (0, 0))
    mine = lambda width: pl.BlockSpec((2 * BLK, width), lambda step, tab_ref: (step, 0))
    return pl.pallas_call(
        finish_kernel,
        out_shape=jax.ShapeDtypeStruct((8 * BLK, 16 * BLK), F32),
        grid_spec=pltpu.PrefetchScalarGridSpec(
            num_scalar_prefetch=1,
            grid=(4,),
            in_specs=[mine(16 * BLK), tiles(True, 0), tiles(True, 1), tiles(False, 0), tiles(False, 1),
                      mine(NPIV)] + [wide] * 4,
            out_specs=mine(16 * BLK),
        ),
        compiler_params=params(),
        name="finish",
    )(tab, parent, arrived, arrived, crossed, crossed, rows, *cols)


def shift(value, axis, size, away):
    return lax.ppermute(value, axis, [(i, (i + away) % size) for i in range(size)])


def gather_front(block, sources=4):
    near = [block]
    for away in range(1, 4):
        near.append(lax.ppermute(block, "x", [(i, (i + away) % 4) for i in range(sources)]))
    return near + [shift(piece, "core", 2, 1) for piece in near]


def row_routes():
    routes = []
    for c in range(16):
        for i in range(8):
            chip = (i // 2 + (c % 8) // 2) % 4
            routes.append((c + 16 * i, c * 8 + chip * 2 + i % 2))
    return routes


def staged(parent_front, child_entries, child_index):
    half, front = lax.axis_index("zh"), lax.axis_index("x") * 2 + lax.axis_index("core")
    pos = jnp.stack([half, lax.axis_index("zl") * 4 + lax.axis_index("y"), front]).astype(jnp.int32)
    tab = make_table(pos, child_index)
    packed = pack_tiles(tab, child_entries)
    arrived = lax.all_to_all(packed, ("zl", "y", "x", "core"), split_axis=0, concat_axis=0, tiled=True)

    strip = make_strip(tab, parent_front, arrived)
    pieces = lax.all_to_all(strip, CUBE, split_axis=0, concat_axis=0, tiled=True)
    summed = pieces[:NPB] + pieces[8:8 + NPB]
    one_block = summed[:, 0].reshape(NPIV, BLK)
    lead_cols = summed[:, 1].reshape(NPIV, BLK)

    along_z = [one_block] + [shift(one_block, ("zh", "zl"), 4, away) for away in range(1, 4)]
    lead_pieces = gather_front(lead_cols, 3)
    moved = lax.ppermute(one_block, CUBE + FRONT, row_routes())
    along_z = jnp.stack(along_z)
    col_pieces = [along_z]
    for away in range(1, 4):
        col_pieces.append(shift(along_z, "y", 4, away))
    row_pieces = gather_front(moved)
    crossed = shift(arrived, "zh", 2, 1)

    inverse = lead_inverse(tab, lead_pieces)
    cols = []
    for away in range(4):
        cols.append(col_panel(inverse, col_pieces[away]))
    rows = row_panel(tab, inverse, row_pieces)
    return finish(tab, parent_front, arrived, crossed, rows, cols)


def solution(mesh):
    split = Mesh(mesh.devices.reshape(2, 2, 4, 4, 2), CUBE + FRONT)
    placed = P(CUBE, FRONT)
    return jax.shard_map(
        staged, mesh=split, in_specs=(placed, placed, P()), out_specs=placed, check_vma=False
    )
```

time: 331 us -> 372 us (1.12)
  starting transfers between devices: 32.6 us -> 135 us
  blocking collectives: 95.5 us -> 61.1 us
  Pallas kernels: 124 us -> 105 us
  between operations: 13.5 us -> 0.24 us
  waiting for transfers between devices: 60.7 us -> 64.9 us
    ppermute x6 -> x22, starting transfers between devices: 32.5 us -> 128 us  [the longest x15 111 us: shift(): lax.ppermute(value, axis, [(i, (i + away) % size) for i in range(size)])]
    all_to_all x2 -> x1, blocking collectives: 95.5 us -> 61.1 us  [staged(): lax.all_to_all(packed, ('zl', 'y', 'x', 'core'), split_axis=0, concat_axi...]
    all_to_all x0 -> x1, waiting for transfers between devices: none -> 28.2 us  [staged(): lax.all_to_all(strip, CUBE, split_axis=0, concat_axis=0, tiled=True)]
    all_gather x2 -> x0, waiting for transfers between devices: 15.3 us -> none  [the longest x1 15.3 us: body(): strips = lax.all_gather(one_block, CUBE, axis=0, tiled=False)]
    pallas_call x1, Pallas kernels: 29.7 us -> 19.6 us  [finish(): pl.pallas_call(finish_kernel, out_shape=jax.ShapeDtypeStruct((8 * BLK, 16...]
    pallas_call x1, Pallas kernels: 51.7 us -> 42.2 us  [lead_inverse(): pl.pallas_call(lead_kernel, out_shape=jax.ShapeDtypeStruct((NPIV, NPIV),...]
    ppermute x6 -> x22, waiting for transfers between devices: 44.7 us -> 36.7 us  [the longest x6 21.3 us: gather_front(): lax.ppermute(block, 'x', [(i, (i + away) % 4) for i in range(sources)])]
    all_to_all x0 -> x1, starting transfers between devices: none -> 6.6 us  [staged(): lax.all_to_all(strip, CUBE, split_axis=0, concat_axis=0, tiled=True)]
  transfers between devices with their start and end apart: 8 -> 23, of which waited for: 5 -> 12; matrix products, arithmetic and copies ran while one was open for 0% -> 0% of each run, Pallas kernels for 25% -> 20%
where the time goes in v2:
time: 372 us; the launch traced here: 371 us
  starting transfers between devices  135 us (36%)
  Pallas kernels  105 us (28%)
  waiting for transfers between devices  64.9 us (17%)
  blocking collectives  61.1 us (16%)
  local copies, waits for them, and re-layouts  4.32 us (1%)
    ppermute x15, starting transfers between devices, shift(): lax.ppermute(value, axis, [(i, (i + away) % size) for i in range(size)])  111 us
    all_to_all x1, blocking collectives, staged(): lax.all_to_all(packed, ('zl', 'y', 'x', 'core'), split_axis=0, concat_axi...  61.1 us
    pallas_call x1, Pallas kernels, lead_inverse(): pl.pallas_call(lead_kernel, out_shape=jax.ShapeDtypeStruct((NPIV, NPIV),...  42.2 us
    all_to_all x1, waiting for transfers between devices, staged(): lax.all_to_all(strip, CUBE, split_axis=0, concat_axis=0, tiled=True)  28.2 us
    ppermute x6, waiting for transfers between devices, gather_front(): lax.ppermute(block, 'x', [(i, (i + away) % 4) for i in range(sources)])  21.3 us
    pallas_call x4, Pallas kernels, col_panel(): pl.pallas_call(col_kernel, out_shape=jax.ShapeDtypeStruct((2 * NPIV, 4 *...  21.1 us
    pallas_call x1, Pallas kernels, finish(): pl.pallas_call(finish_kernel, out_shape=jax.ShapeDtypeStruct((8 * BLK, 16...  19.6 us
    ppermute x6, starting transfers between devices, gather_front(): lax.ppermute(block, 'x', [(i, (i + away) % 4) for i in range(sources)])  17.1 us
  transfers between devices with their start and end apart: 23, of which 12 were waited for; matrix products, arithmetic and copies ran while one was open for 0% of the time, Pallas kernels for 20%

profile of v2, /device:TPU:0, one launch (start us, length us, event | category | flops | bytes accessed | tf_op | source)
XLA Modules:
  0.0 370.8 jit_solution(12436485835585827044)
XLA Ops:
  2.2 7.4 %pack_tiles.1 = f32[64,128,128]{2,1,0:T(8,128)} custom-call(s32[64]{0:T(128)} %make_table.1.tab_ref, f32[1024,1024]{1,0:T(8,128)} %tile_ref.1), custom_call_target="tpu_custom_call" | custom-call | tf_op jit(solution)/shard_map/pack_tiles/pallas_call | solution.py:75
  9.6 61.1 %all_to_all.10.tile_ref.own0.own1 = f32[64,128,128]{2,1,0:T(8,128)} all-to-all(f32[64,128,128]{2,1,0:T(8,128)} %pack_tiles.1), channel_id=1, replica_groups=mesh['zh'=2,'zl'=2,'y'=4,'x'=4,'core'=2] {'zl','y','x','core'}, dimensions={0} | all-to-all | bytes 8388608 | tf_op jit(solution)/shard_map/all_to_all | solution.py:404
  70.7 3.6 make_strip.1
  74.3 6.6 %all-to-all-start.1 = ((f32[16,2,128,128]{3,2,1,0:T(8,128)}), f32[16,2,128,128]{3,2,1,0:T(8,128)S(1)}, u32[]{:S(2)}, u32[]{:S(2)}) async-start(f32[16,2,128,128]{3,2,1,0:T(8,128)} %make_strip.1), calls=%async_computation.1 | async-start | bytes 4194304 | tf_op jit(solution)/shard_map/all_to_all | solution.py:407
  80.9 3.4 collective-permute-start
  84.3 28.2 %all-to-all-done.1 = f32[16,2,128,128]{3,2,1,0:T(8,128)S(1)} async-done(((f32[16,2,128,128]{3,2,1,0:T(8,128)}), f32[16,2,128,128]{3,2,1,0:T(8,128)S(1)}, u32[]{:S(2)}, u32[]{:S(2)}) %all-to-all-start.1) | async-done | bytes 2097184 | tf_op jit(solution)/shard_map/all_to_all | solution.py:407
  113.3 92.7 %collective-permute-start.17 = (f32[768,128]{1,0:T(8,128)S(1)}, f32[768,128]{1,0:T(8,128)S(1)}, u32[]{:S(2)}, u32[]{:S(2)}) collective-permute-start(f32[768,128]{1,0:T(8,128)S(1)} %bitcast.15), channel_id=1, source_target_pairs={{0,64},{32,96},{64,0},{96,32},{1,65},{33,97},{65,1},{97,33},{2,66}... | collective-permute-start | bytes 1179656 | tf_op jit(solution)/shard_map/ppermute | solution.py:380
  209.1 4.3 %collective-permute-done.17 = f32[768,128]{1,0:T(8,128)S(1)} collective-permute-done((f32[768,128]{1,0:T(8,128)S(1)}, f32[768,128]{1,0:T(8,128)S(1)}, u32[]{:S(2)}, u32[]{:S(2)}) %collective-permute-start.17) | collective-permute-done | bytes 393248 | tf_op jit(solution)/shard_map/ppermute | solution.py:380
  216.6 3.2 collective-permute-done.16
  219.8 4.9 %collective-permute-start.2 = (f32[768,128]{1,0:T(8,128)S(1)}, f32[768,128]{1,0:T(8,128)S(1)}, u32[]{:S(2)}, u32[]{:S(2)}) collective-permute-start(f32[768,128]{1,0:T(8,128)S(1)} %bitcast.11), channel_id=1, source_target_pairs={{0,4},{2,6},{4,0},{1,5},{3,7},{5,1},{8,12},{10,14},{12,8},{9,13},{... | collective-permute-start | bytes 1179656 | tf_op jit(solution)/shard_map/ppermute | solution.py:386
  224.7 3.2 collective-permute-start.1
  229.3 4.6 %collective-permute-done.2.refs_2_ = f32[768,128]{1,0:T(8,128)S(1)} collective-permute-done((f32[768,128]{1,0:T(8,128)S(1)}, f32[768,128]{1,0:T(8,128)S(1)}, u32[]{:S(2)}, u32[]{:S(2)}) %collective-permute-start.2) | collective-permute-done | bytes 393248 | tf_op jit(solution)/shard_map/ppermute | solution.py:386
  236.1 4.4 %collective-permute-done.1.refs_1_ = f32[768,128]{1,0:T(8,128)S(1)} collective-permute-done((f32[768,128]{1,0:T(8,128)S(1)}, f32[768,128]{1,0:T(8,128)S(1)}, u32[]{:S(2)}, u32[]{:S(2)}) %collective-permute-start.1) | collective-permute-done | bytes 393248 | tf_op jit(solution)/shard_map/ppermute | solution.py:386
  244.4 6.4 %collective-permute-done.10.refs_2_ = f32[768,128]{1,0:T(8,128)S(1)} collective-permute-done((f32[768,128]{1,0:T(8,128)S(1)}, f32[768,128]{1,0:T(8,128)S(1)}, u32[]{:S(2)}, u32[]{:S(2)}) %collective-permute-start.10) | collective-permute-done | bytes 393248 | tf_op jit(solution)/shard_map/ppermute | solution.py:386
  251.0 4.5 %collective-permute-done.9.refs_1_ = f32[768,128]{1,0:T(8,128)S(1)} collective-permute-done((f32[768,128]{1,0:T(8,128)S(1)}, f32[768,128]{1,0:T(8,128)S(1)}, u32[]{:S(2)}, u32[]{:S(2)}) %collective-permute-start.9) | collective-permute-done | bytes 393248 | tf_op jit(solution)/shard_map/ppermute | solution.py:386
  255.5 9.0 %collective-permute-start.21 = (f32[4,768,128]{2,1,0:T(8,128)S(1)}, f32[4,768,128]{2,1,0:T(8,128)S(1)}, u32[]{:S(2)}, u32[]{:S(2)}) collective-permute-start(f32[4,768,128]{2,1,0:T(8,128)S(1)} %pad_maximum_fusion.strip_ref), channel_id=1, source_target_pairs={{0,24},{8,0},{16,8},{24,16},{1,25},{9,1},{17,9},{25,17},{2,26},{10... | collective-permute-start | bytes 4718600 | tf_op jit(solution)/shard_map/ppermute | solution.py:380
  271.2 42.2 %lead_inverse.1.inverse_ref = f32[768,768]{1,0:T(8,128)} custom-call(s32[64]{0:T(128)} %make_table.1.tab_ref, f32[768,128]{1,0:T(8,128)} %bitcast.13, f32[768,128]{1,0:T(8,128)} %copy-done.16, f32[768,128]{1,0:T(8,128)} %copy-done.15, f32[768,128]{1,0:T(8,128)} %copy-done.14, f32[768,128]{1,0:T(8,128)} %copy-done.13, f32[768,128]{1,0:T(8,128)} %copy-done.17, ...), custom_call_target="tpu_custom_call" | custom-call | tf_op jit(solution)/shard_map/lead_inverse/pallas_call | solution.py:232
  313.4 5.3 %col_panel.4.refs_0_ = bf16[1536,512]{1,0:T(8,128)(2,1)} custom-call(f32[768,768]{1,0:T(8,128)} %lead_inverse.1.inverse_ref, f32[4,768,128]{2,1,0:T(8,128)} %copy-done), custom_call_target="tpu_custom_call" | custom-call | tf_op jit(solution)/shard_map/col_panel/pallas_call | solution.py:275
  319.5 9.0 %row_panel.1.rows_ref = f32[1024,768]{1,0:T(8,128)} custom-call(s32[64]{0:T(128)} %make_table.1.tab_ref, f32[768,768]{1,0:T(8,128)} %lead_inverse.1.inverse_ref, f32[768,128]{1,0:T(8,128)} %copy-done.5, f32[768,128]{1,0:T(8,128)} %copy-done.9, f32[768,128]{1,0:T(8,128)} %copy-done.8, f32[768,128]{1,0:T(8,128)} %copy-done.7, f32[768,128]{1,0:T(8,128)} %copy-done.6, ...), custom_call_target="tpu_custom_call" | custom-call | tf_op jit(solution)/shard_map/row_panel/pallas_call | solution.py:297
  328.6 3.4 collective-permute-done.21.strip_ref
  333.1 5.3 %col_panel.7.refs_3_ = bf16[1536,512]{1,0:T(8,128)(2,1)} custom-call(f32[768,768]{1,0:T(8,128)} %lead_inverse.1.inverse_ref, f32[4,768,128]{2,1,0:T(8,128)} %copy-done.2), custom_call_target="tpu_custom_call" | custom-call | tf_op jit(solution)/shard_map/col_panel/pallas_call | solution.py:275
  339.6 5.3 %col_panel.6.refs_2_ = bf16[1536,512]{1,0:T(8,128)(2,1)} custom-call(f32[768,768]{1,0:T(8,128)} %lead_inverse.1.inverse_ref, f32[4,768,128]{2,1,0:T(8,128)} %copy-done.3), custom_call_target="tpu_custom_call" | custom-call | tf_op jit(solution)/shard_map/col_panel/pallas_call | solution.py:275
  346.0 5.3 %col_panel.5.refs_1_ = bf16[1536,512]{1,0:T(8,128)(2,1)} custom-call(f32[768,768]{1,0:T(8,128)} %lead_inverse.1.inverse_ref, f32[4,768,128]{2,1,0:T(8,128)} %copy-done.4), custom_call_target="tpu_custom_call" | custom-call | tf_op jit(solution)/shard_map/col_panel/pallas_call | solution.py:275
  351.2 19.6 %finish.1 = f32[1024,2048]{1,0:T(8,128)} custom-call(s32[64]{0:T(128)} %make_table.1.tab_ref, f32[1024,2048]{1,0:T(8,128)} %parent_ref.3, f32[64,128,128]{2,1,0:T(8,128)} %all_to_all.10.tile_ref.own0.own1, f32[64,128,128]{2,1,0:T(8,128)} %all_to_all.10.tile_ref.own0.own1, f32[64,128,128]{2,1,0:T(8,128)} %collective-permute-done.other0.other1, ...), custom_call_target="tpu_custom_call" | custom-call | tf_op jit(solution)/shard_map/finish/pallas_call | solution.py:364
  (73 shorter events, 27.6 us)
Async XLA Ops:
  74.3 38.2 %all-to-all-start.1 = ((f32[16,2,128,128]{3,2,1,0:T(8,128)}), f32[16,2,128,128]{3,2,1,0:T(8,128)S(1)}, u32[]{:S(2)}, u32[]{:S(2)}) async-start(f32[16,2,128,128]{3,2,1,0:T(8,128)} %make_strip.1), calls=%async_computation.1 | async-start | bytes 4194304 | tf_op jit(solution)/shard_map/all_to_all | solution.py:407
  80.9 270.3 %collective-permute-start = (f32[64,128,128]{2,1,0:T(8,128)}, f32[64,128,128]{2,1,0:T(8,128)}, u32[]{:S(2)}, u32[]{:S(2)}) collective-permute-start(f32[64,128,128]{2,1,0:T(8,128)} %all_to_all.10.tile_ref.own0.own1), channel_id=1, source_target_pairs={{0,64},{64,0},{1,65},{65,1},{2,66},{66,2},{3,67},{67,3},{4,68},{68... | collective-permute-start | bytes 12582920 | tf_op jit(solution)/shard_map/ppermute | solution.py:380
  112.7 138.2 %copy-start.1 = (f32[6,1,128,128]{3,2,1,0:T(8,128)}, f32[6,1,128,128]{3,2,1,0:T(8,128)S(1)}, u32[]{:S(2)}) copy-start(f32[6,1,128,128]{3,2,1,0:T(8,128)S(1)} %get-tuple-element.6) | copy-start | bytes 1179652
  112.7 96.5 %collective-permute-start.18 = (f32[768,128]{1,0:T(8,128)S(1)}, f32[768,128]{1,0:T(8,128)S(1)}, u32[]{:S(2)}, u32[]{:S(2)}) collective-permute-start(f32[768,128]{1,0:T(8,128)S(1)} %bitcast.14), channel_id=1, source_target_pairs={{0,96},{32,0},{64,32},{96,64},{1,97},{33,1},{65,33},{97,65},{2,98}... | collective-permute-start | bytes 1179656 | tf_op jit(solution)/shard_map/ppermute | solution.py:380
  113.3 100.1 %collective-permute-start.17 = (f32[768,128]{1,0:T(8,128)S(1)}, f32[768,128]{1,0:T(8,128)S(1)}, u32[]{:S(2)}, u32[]{:S(2)}) collective-permute-start(f32[768,128]{1,0:T(8,128)S(1)} %bitcast.15), channel_id=1, source_target_pairs={{0,64},{32,96},{64,0},{96,32},{1,65},{33,97},{65,1},{97,33},{2,66}... | collective-permute-start | bytes 1179656 | tf_op jit(solution)/shard_map/ppermute | solution.py:380
  206.0 13.8 %collective-permute-start.16 = (f32[768,128]{1,0:T(8,128)S(1)}, f32[768,128]{1,0:T(8,128)S(1)}, u32[]{:S(2)}, u32[]{:S(2)}) collective-permute-start(f32[768,128]{1,0:T(8,128)S(1)} %bitcast.16), channel_id=1, source_target_pairs={{0,32},{32,64},{64,96},{96,0},{1,33},{33,65},{65,97},{97,1},{2,34}... | collective-permute-start | bytes 1179656 | tf_op jit(solution)/shard_map/ppermute | solution.py:380
  207.4 17.4 %collective-permute-start.8 = (f32[768,128]{1,0:T(8,128)S(1)}, f32[768,128]{1,0:T(8,128)S(1)}, u32[]{:S(2)}, u32[]{:S(2)}) collective-permute-start(f32[768,128]{1,0:T(8,128)S(1)} %bitcast.17), channel_id=1, source_target_pairs={{0,0},{16,1},{32,2},{48,3},{64,4},{80,5},{96,6},{112,7},{1,8},{17,... | collective-permute-start | bytes 1179656 | tf_op jit(solution)/shard_map/ppermute | solution.py:414
  209.1 18.9 %collective-permute-start.4 = (f32[768,128]{1,0:T(8,128)S(1)}, f32[768,128]{1,0:T(8,128)S(1)}, u32[]{:S(2)}, u32[]{:S(2)}) collective-permute-start(f32[768,128]{1,0:T(8,128)S(1)} %bitcast.9), channel_id=1, source_target_pairs={{0,1},{1,0},{2,3},{3,2},{4,5},{5,4},{6,7},{7,6},{8,9},{9,8},{10,11... | collective-permute-start | bytes 1179656 | tf_op jit(solution)/shard_map/ppermute | solution.py:380
  213.5 14.6 %collective-permute-start.3 = (f32[768,128]{1,0:T(8,128)S(1)}, f32[768,128]{1,0:T(8,128)S(1)}, u32[]{:S(2)}, u32[]{:S(2)}) collective-permute-start(f32[768,128]{1,0:T(8,128)S(1)} %bitcast.10), channel_id=1, source_target_pairs={{0,6},{2,0},{4,2},{1,7},{3,1},{5,3},{8,14},{10,8},{12,10},{9,15},{... | collective-permute-start | bytes 1179656 | tf_op jit(solution)/shard_map/ppermute | solution.py:386
  219.8 14.1 %collective-permute-start.2 = (f32[768,128]{1,0:T(8,128)S(1)}, f32[768,128]{1,0:T(8,128)S(1)}, u32[]{:S(2)}, u32[]{:S(2)}) collective-permute-start(f32[768,128]{1,0:T(8,128)S(1)} %bitcast.11), channel_id=1, source_target_pairs={{0,4},{2,6},{4,0},{1,5},{3,7},{5,1},{8,12},{10,14},{12,8},{9,13},{... | collective-permute-start | bytes 1179656 | tf_op jit(solution)/shard_map/ppermute | solution.py:386
  224.7 15.8 %collective-permute-start.1 = (f32[768,128]{1,0:T(8,128)S(1)}, f32[768,128]{1,0:T(8,128)S(1)}, u32[]{:S(2)}, u32[]{:S(2)}) collective-permute-start(f32[768,128]{1,0:T(8,128)S(1)} %bitcast.12), channel_id=1, source_target_pairs={{0,2},{2,4},{4,6},{1,3},{3,5},{5,7},{8,10},{10,12},{12,14},{9,11},... | collective-permute-start | bytes 1179656 | tf_op jit(solution)/shard_map/ppermute | solution.py:386
  228.0 15.0 %collective-permute-start.12 = (f32[768,128]{1,0:T(8,128)S(1)}, f32[768,128]{1,0:T(8,128)S(1)}, u32[]{:S(2)}, u32[]{:S(2)}) collective-permute-start(f32[768,128]{1,0:T(8,128)S(1)} %collective-permute-done.8.refs_0_), channel_id=1, source_target_pairs={{0,1},{1,0},{2,3},{3,2},{4,5},{5,4},{6,7},{7,6},{8,9},{9,8},{10,11... | collective-permute-start | bytes 1179656 | tf_op jit(solution)/shard_map/ppermute | solution.py:380
  228.1 16.3 %collective-permute-start.11 = (f32[768,128]{1,0:T(8,128)S(1)}, f32[768,128]{1,0:T(8,128)S(1)}, u32[]{:S(2)}, u32[]{:S(2)}) collective-permute-start(f32[768,128]{1,0:T(8,128)S(1)} %collective-permute-done.8.refs_0_), channel_id=1, source_target_pairs={{0,6},{2,0},{4,2},{6,4},{1,7},{3,1},{5,3},{7,5},{8,14},{10,8},{12,... | collective-permute-start | bytes 1179656 | tf_op jit(solution)/shard_map/ppermute | solution.py:386
  233.9 16.9 %collective-permute-start.10 = (f32[768,128]{1,0:T(8,128)S(1)}, f32[768,128]{1,0:T(8,128)S(1)}, u32[]{:S(2)}, u32[]{:S(2)}) collective-permute-start(f32[768,128]{1,0:T(8,128)S(1)} %collective-permute-done.8.refs_0_), channel_id=1, source_target_pairs={{0,4},{2,6},{4,0},{6,2},{1,5},{3,7},{5,1},{7,3},{8,12},{10,14},{12... | collective-permute-start | bytes 1179656 | tf_op jit(solution)/shard_map/ppermute | solution.py:386
  240.5 15.0 %collective-permute-start.9 = (f32[768,128]{1,0:T(8,128)S(1)}, f32[768,128]{1,0:T(8,128)S(1)}, u32[]{:S(2)}, u32[]{:S(2)}) collective-permute-start(f32[768,128]{1,0:T(8,128)S(1)} %collective-permute-done.8.refs_0_), channel_id=1, source_target_pairs={{0,2},{2,4},{4,6},{6,0},{1,3},{3,5},{5,7},{7,1},{8,10},{10,12},{12... | collective-permute-start | bytes 1179656 | tf_op jit(solution)/shard_map/ppermute | solution.py:386
  243.0 21.6 %collective-permute-start.7 = (f32[768,128]{1,0:T(8,128)S(1)}, f32[768,128]{1,0:T(8,128)}, u32[]{:S(2)}, u32[]{:S(2)}) collective-permute-start(f32[768,128]{1,0:T(8,128)S(1)} %collective-permute-done.3.refs_3_), channel_id=1, source_target_pairs={{0,1},{1,0},{2,3},{3,2},{4,5},{5,4},{6,7},{7,6},{8,9},{9,8},{10,11... | collective-permute-start | bytes 1179656 | tf_op jit(solution)/shard_map/ppermute | solution.py:380
  244.4 21.6 %collective-permute-start.6 = (f32[768,128]{1,0:T(8,128)S(1)}, f32[768,128]{1,0:T(8,128)}, u32[]{:S(2)}, u32[]{:S(2)}) collective-permute-start(f32[768,128]{1,0:T(8,128)S(1)} %collective-permute-done.2.refs_2_), channel_id=1, source_target_pairs={{0,1},{1,0},{2,3},{3,2},{4,5},{5,4},{6,7},{7,6},{8,9},{9,8},{10,11... | collective-permute-start | bytes 1179656 | tf_op jit(solution)/shard_map/ppermute | solution.py:380
  250.8 16.6 %collective-permute-start.5 = (f32[768,128]{1,0:T(8,128)S(1)}, f32[768,128]{1,0:T(8,128)S(1)}, u32[]{:S(2)}, u32[]{:S(2)}) collective-permute-start(f32[768,128]{1,0:T(8,128)S(1)} %collective-permute-done.1.refs_1_), channel_id=1, source_target_pairs={{0,1},{1,0},{2,3},{3,2},{4,5},{5,4},{6,7},{7,6},{8,9},{9,8},{10,11... | collective-permute-start | bytes 1179656 | tf_op jit(solution)/shard_map/ppermute | solution.py:380
  255.5 76.5 %collective-permute-start.21 = (f32[4,768,128]{2,1,0:T(8,128)S(1)}, f32[4,768,128]{2,1,0:T(8,128)S(1)}, u32[]{:S(2)}, u32[]{:S(2)}) collective-permute-start(f32[4,768,128]{2,1,0:T(8,128)S(1)} %pad_maximum_fusion.strip_ref), channel_id=1, source_target_pairs={{0,24},{8,0},{16,8},{24,16},{1,25},{9,1},{17,9},{25,17},{2,26},{10... | collective-permute-start | bytes 4718600 | tf_op jit(solution)/shard_map/ppermute | solution.py:380
  264.5 73.9 %collective-permute-start.20 = (f32[4,768,128]{2,1,0:T(8,128)S(1)}, f32[4,768,128]{2,1,0:T(8,128)S(1)}, u32[]{:S(2)}, u32[]{:S(2)}) collective-permute-start(f32[4,768,128]{2,1,0:T(8,128)S(1)} %pad_maximum_fusion.strip_ref), channel_id=1, source_target_pairs={{0,16},{8,24},{16,0},{24,8},{1,17},{9,25},{17,1},{25,9},{2,18},{10... | collective-permute-start | bytes 4718600 | tf_op jit(solution)/shard_map/ppermute | solution.py:380
  266.1 78.8 %collective-permute-start.19 = (f32[4,768,128]{2,1,0:T(8,128)S(1)}, f32[4,768,128]{2,1,0:T(8,128)S(1)}, u32[]{:S(2)}, u32[]{:S(2)}) collective-permute-start(f32[4,768,128]{2,1,0:T(8,128)S(1)} %pad_maximum_fusion.strip_ref), channel_id=1, source_target_pairs={{0,8},{8,16},{16,24},{24,0},{1,9},{9,17},{17,25},{25,1},{2,10},{10... | collective-permute-start | bytes 4718600 | tf_op jit(solution)/shard_map/ppermute | solution.py:380
  267.4 1.8 collective-permute-start.15
  269.2 1.7 collective-permute-start.14
  270.9 47.8 %collective-permute-start.13 = (f32[768,128]{1,0:T(8,128)S(1)}, f32[768,128]{1,0:T(8,128)S(1)}, u32[]{:S(2)}, u32[]{:S(2)}) collective-permute-start(f32[768,128]{1,0:T(8,128)S(1)} %collective-permute-done.9.refs_1_), channel_id=1, source_target_pairs={{0,1},{1,0},{2,3},{3,2},{4,5},{5,4},{6,7},{7,6},{8,9},{9,8},{10,11... | collective-permute-start | bytes 1179656 | tf_op jit(solution)/shard_map/ppermute | solution.py:380
  (17 other events, 383.5 us)

commit v3 on v2

--- a/solution.py
+++ b/solution.py
@@ -24,7 +24,9 @@
 COL_PICK = 40
 PIVOT = 48
 HALF, RES, FRONT_AT = 50, 51, 52
-SPARE = 53
+CROSS = 53
+CROSSINGS = 61
+SPARE = 62
 TABLE = 64
 
 
@@ -49,6 +51,16 @@
             tab_ref[jnp.where(mine, GROUP + child_id * 8 + (row >> 4), SPARE)] = jnp.int32(run)
             tab_ref[jnp.where(row == res, PIVOT + child_id, SPARE)] = jnp.int32(run)
             tab_ref[COLUMN + child_id * 8 + run] = col >> 3
+    count = jnp.int32(0)
+    last = jnp.int32(0)
+    for i in range(8):
+        hit = tab_ref[GROUP + (1 - half) * 8 + i] >= 0
+        tab_ref[jnp.where(hit, CROSS + count, SPARE)] = jnp.int32(i)
+        last = jnp.where(hit, i, last)
+        count = count + jnp.where(hit, 1, 0)
+    for i in range(8):
+        tab_ref[CROSS + i] = jnp.where(i < count, tab_ref[CROSS + i], last)
+    tab_ref[CROSSINGS] = count
     for u in range(8):
         tab_ref[ROW_PICK + (idx_ref[half, res * 8 + u] & 7)] = jnp.int32(u)
         tab_ref[COL_PICK + (idx_ref[half, front * 8 + u] & 7)] = jnp.int32(u)
@@ -65,10 +77,11 @@
     )(pos, idx)
 
 
-def pack_kernel(tab_ref, tile_ref, out_ref):
+def pack_kernel(tab_ref, even_ref, odd_ref, out_ref):
     for dest in range(8):
         col = pl.multiple_of(tab_ref[COL_PICK + dest] * BLK, BLK)
-        out_ref[dest] = tile_ref[:, pl.ds(col, BLK)]
+        out_ref[dest] = even_ref[:, pl.ds(col, BLK)]
+        out_ref[8 + dest] = odd_ref[:, pl.ds(col, BLK)]
 
 
 def pack_tiles(tab, child):
@@ -77,13 +90,16 @@
         out_shape=jax.ShapeDtypeStruct((64, BLK, BLK), F32),
         grid_spec=pltpu.PrefetchScalarGridSpec(
             num_scalar_prefetch=1,
-            grid=(8,),
-            in_specs=[pl.BlockSpec((BLK, 8 * BLK), lambda step, tab_ref: (tab_ref[ROW_PICK + step], 0))],
-            out_specs=pl.BlockSpec((8, BLK, BLK), lambda step, tab_ref: (step, 0, 0)),
+            grid=(4,),
+            in_specs=[
+                pl.BlockSpec((BLK, 8 * BLK), lambda step, tab_ref: (tab_ref[ROW_PICK + 2 * step], 0)),
+                pl.BlockSpec((BLK, 8 * BLK), lambda step, tab_ref: (tab_ref[ROW_PICK + 2 * step + 1], 0)),
+            ],
+            out_specs=pl.BlockSpec((16, BLK, BLK), lambda step, tab_ref: (step, 0, 0)),
         ),
         compiler_params=params(),
         name="pack_tiles",
-    )(tab, child)
+    )(tab, child, child)
 
 
 def strip_kernel(tab_ref, parent_ref, tile_ref, out_ref):
@@ -188,7 +204,7 @@
 
 
 def lead_kernel(tab_ref, *refs):
-    pieces, (out_ref, work_ref, d_ref, b_ref) = refs[:8], refs[8:]
+    pieces, (high_ref, low_ref, work_ref, d_ref, b_ref) = refs[:8], refs[8:]
     chip, core = tab_ref[FRONT_AT] // 2, lax.rem(tab_ref[FRONT_AT], 2)
     for away in range(4):
         source = lax.rem(chip + 4 - away, 4)
@@ -225,18 +241,21 @@
         return carry
 
     lax.fori_loop(0, NPB, eliminate, 0)
-    out_ref[...] = work_ref[:, NPIV:]
+    inverse = work_ref[:, NPIV:]
+    high, low = halves(inverse)
+    high_ref[...] = high
+    low_ref[...] = low
 
 
 def lead_inverse(tab, pieces):
     return pl.pallas_call(
         lead_kernel,
-        out_shape=jax.ShapeDtypeStruct((NPIV, NPIV), F32),
+        out_shape=(jax.ShapeDtypeStruct((NPIV, NPIV), jnp.bfloat16),) * 2,
         grid_spec=pltpu.PrefetchScalarGridSpec(
             num_scalar_prefetch=1,
             grid=(1,),
             in_specs=[pl.BlockSpec((NPIV, BLK), lambda step, tab_ref: (0, 0))] * 8,
-            out_specs=pl.BlockSpec((NPIV, NPIV), lambda step, tab_ref: (0, 0)),
+            out_specs=(pl.BlockSpec((NPIV, NPIV), lambda step, tab_ref: (0, 0)),) * 2,
             scratch_shapes=[
                 pltpu.VMEM((NPIV, 2 * NPIV), F32),
                 pltpu.VMEM((BLK, BLK), F32),
@@ -259,34 +278,47 @@
     return product + jnp.dot(left[0], right[0], preferred_element_type=F32)
 
 
+def lower_dot(left, right):
+    step = 2 * BLK
+    bands = []
+    for at in range(0, NPIV, step):
+        rows, cols = slice(at, at + step), slice(0, at + step)
+        bands.append(dot_halves([part[rows, cols] for part in left], [part[cols] for part in right]))
+    return jnp.concatenate(bands, axis=0)
+
+
 def whole(*shape):
     return pl.BlockSpec(shape, lambda step, tab_ref: (0,) * len(shape))
 
 
-def col_kernel(inverse_ref, strip_ref, out_ref):
-    inverse = halves(inverse_ref[...])
-    strip = jnp.concatenate([strip_ref[0], strip_ref[1], strip_ref[2], strip_ref[3]], axis=1)
-    high, low = halves(dot_halves(inverse, halves(strip)))
+def col_kernel(high_in, low_in, *refs):
+    strip_refs, out_ref = refs[:-1], refs[-1]
+    inverse = high_in[...], low_in[...]
+    blocks = []
+    for ref in strip_refs:
+        blocks += [ref[...]] if ref.shape == (NPIV, BLK) else [ref[part] for part in range(ref.shape[0])]
+    high, low = halves(lower_dot(inverse, halves(jnp.concatenate(blocks, axis=1))))
     out_ref[:NPIV, :] = low
     out_ref[NPIV:, :] = high
 
 
-def col_panel(inverse, piece):
+def col_panel(inverse, pieces):
+    count = sum(piece.size for piece in pieces) // (NPIV * BLK)
     return pl.pallas_call(
         col_kernel,
-        out_shape=jax.ShapeDtypeStruct((2 * NPIV, 4 * BLK), jnp.bfloat16),
+        out_shape=jax.ShapeDtypeStruct((2 * NPIV, count * BLK), jnp.bfloat16),
         compiler_params=params(),
         name="col_panel",
-    )(inverse, piece)
-
-
-def row_kernel(tab_ref, inverse_ref, *refs):
+    )(*inverse, *pieces)
+
+
+def row_kernel(tab_ref, high_in, low_in, *refs):
     row_refs, rows_ref = refs[:8], refs[8]
     chip, core = tab_ref[FRONT_AT] // 2, lax.rem(tab_ref[FRONT_AT], 2)
-    inverse = halves(inverse_ref[...])
+    inverse = high_in[...], low_in[...]
     for away in range(4):
         strip = jnp.concatenate([row_refs[away][...], row_refs[4 + away][...]], axis=1)
-        panel = dot_halves(inverse, halves(strip)).T
+        panel = lower_dot(inverse, halves(strip)).T
         pair = lax.rem(chip + 8 - away - tab_ref[RES] // 2, 4)
         for other in range(2):
             at = (pair * 2 + lax.rem(core + other, 2)) * BLK
@@ -300,44 +332,50 @@
         grid_spec=pltpu.PrefetchScalarGridSpec(
             num_scalar_prefetch=1,
             grid=(1,),
-            in_specs=[whole(NPIV, NPIV)] + [whole(NPIV, BLK)] * 8,
+            in_specs=[whole(NPIV, NPIV)] * 2 + [whole(NPIV, BLK)] * 8,
             out_specs=whole(8 * BLK, NPIV),
         ),
         compiler_params=params(),
         name="row_panel",
-    )(tab, inverse, *pieces)
-
-
-def slot_col(tab_ref, slot):
-    z = tab_ref[HALF] * 2 + tab_ref[RES] // 4
-    y = lax.rem(tab_ref[RES], 4)
-    return lax.rem(z + 4 - slot % 4, 4) * 4 + lax.rem(y + 4 - slot // 4, 4)
-
-
-def finish_kernel(tab_ref, parent_ref, own0, own1, other0, other1, rows_ref, *refs):
-    col_refs, out_ref = refs[:4], refs[4]
+    )(tab, *inverse, *pieces)
+
+
+SLOTS = [
+    [(0, away) for away in range(4)] + [(deep, 0) for deep in range(1, 4)],
+    [(deep, away) for away in (1, 3) for deep in range(1, 4)],
+    [(deep, 2) for deep in range(1, 4)],
+]
+
+
+def slot_col(tab_ref, deep, away):
+    z = tab_ref[HALF] * 2 + (tab_ref[RES] >> 2)
+    y = tab_ref[RES] & 3
+    return ((z + 4 - deep) & 3) * 4 + ((y + 4 - away) & 3)
+
+
+def finish_kernel(tab_ref, parent_ref, own0, own1, rows_ref, *refs):
+    col_refs, out_ref = refs[:-1], refs[-1]
     half, res, front = tab_ref[HALF], tab_ref[RES], tab_ref[FRONT_AT]
     step = pl.program_id(0)
     high, low = halves(rows_ref[...])
     both = jnp.concatenate([high, low], axis=1)
-    for away in range(4):
-        product = jnp.dot(both, col_refs[away][...], preferred_element_type=F32)
-        product = product + jnp.dot(high, col_refs[away][NPIV:, :], preferred_element_type=F32)
-        for part in range(4):
-            at = pl.ds(pl.multiple_of(slot_col(tab_ref, 4 * away + part) * BLK, BLK), BLK)
+    for slots, ref in zip(SLOTS, col_refs):
+        product = jnp.dot(both, ref[...], preferred_element_type=F32)
+        product = product + jnp.dot(high, ref[NPIV:, :], preferred_element_type=F32)
+        for part, place in enumerate(slots):
+            at = pl.ds(pl.multiple_of(slot_col(tab_ref, *place) * BLK, BLK), BLK)
             out_ref[:, at] = parent_ref[:, at] - product[:, part * BLK:(part + 1) * BLK]
-    for part, tile_refs in enumerate(((own0, other0), (own1, other1))):
+    for part, tiles in enumerate((own0, own1)):
         row_block = half * 8 + res + 16 * (2 * step + part)
         rows = slice(part * BLK, (part + 1) * BLK)
-        for child_id, tiles in ((half, tile_refs[0]), (1 - half, tile_refs[1])):
-            group = tab_ref[GROUP + child_id * 8 + 2 * step + part]
-
-            @pl.when(group >= 0)
-            def _():
-                for source in range(8):
-                    col = tab_ref[COLUMN + child_id * 8 + source]
-                    at = pl.ds(pl.multiple_of(col * BLK, BLK), BLK)
-                    out_ref[rows, at] = out_ref[rows, at] + tiles[source]
+        group = tab_ref[GROUP + half * 8 + 2 * step + part]
+
+        @pl.when(group >= 0)
+        def _():
+            for source in range(8):
+                col = tab_ref[COLUMN + half * 8 + source]
+                at = pl.ds(pl.multiple_of(col * BLK, BLK), BLK)
+                out_ref[rows, at] = out_ref[rows, at] + tiles[source]
 
         @pl.when(row_block < NPB)
         def _():
@@ -351,15 +389,14 @@
             out_ref[rows, :BLK] = jnp.where(row_id >= col_id, rows_ref[rows, pl.ds(lane, BLK)], 0.0)
 
 
-def finish(tab, parent, arrived, crossed, rows, cols):
-    def tiles(own, part):
+def finish(tab, parent, arrived, rows, cols):
+    def tiles(part):
         def pick(step, tab_ref):
-            child_id = tab_ref[HALF] if own else 1 - tab_ref[HALF]
-            return (lax.max(tab_ref[GROUP + child_id * 8 + 2 * step + part], 0), 0, 0)
+            return (lax.max(tab_ref[GROUP + tab_ref[HALF] * 8 + 2 * step + part], 0), 0, 0)
 
         return pl.BlockSpec((8, BLK, BLK), pick)
 
-    wide = pl.BlockSpec((2 * NPIV, 4 * BLK), lambda step, tab_ref: (0, 0))
+    wide = [pl.BlockSpec((2 * NPIV, len(slots) * BLK), lambda step, tab_ref: (0, 0)) for slots in SLOTS]
     mine = lambda width: pl.BlockSpec((2 * BLK, width), lambda step, tab_ref: (step, 0))
     return pl.pallas_call(
         finish_kernel,
@@ -367,13 +404,55 @@
         grid_spec=pltpu.PrefetchScalarGridSpec(
             num_scalar_prefetch=1,
             grid=(4,),
-            in_specs=[mine(16 * BLK), tiles(True, 0), tiles(True, 1), tiles(False, 0), tiles(False, 1),
-                      mine(NPIV)] + [wide] * 4,
+            in_specs=[mine(16 * BLK), tiles(0), tiles(1), mine(NPIV)] + wide,
             out_specs=mine(16 * BLK),
         ),
         compiler_params=params(),
         name="finish",
-    )(tab, parent, arrived, arrived, crossed, crossed, rows, *cols)
+    )(tab, parent, arrived, arrived, rows, *cols)
+
+
+def enter_kernel(tab_ref, front_ref, tile_ref, out_ref):
+    half, front = tab_ref[HALF], tab_ref[FRONT_AT]
+    step = pl.program_id(0)
+    count = tab_ref[CROSSINGS]
+
+    @pl.when(step < lax.max(count, 1))
+    def _():
+        out_ref[...] = front_ref[...]
+
+    row_block = half * 8 + tab_ref[RES] + 16 * tab_ref[CROSS + step]
+
+    @pl.when((step < count) & (row_block >= NPB))
+    def _():
+        for source in range(8):
+            col = tab_ref[COLUMN + (1 - half) * 8 + source]
+
+            @pl.when(front + 8 * col >= NPB)
+            def _():
+                at = pl.ds(pl.multiple_of(col * BLK, BLK), BLK)
+                out_ref[:, at] = out_ref[:, at] + tile_ref[source]
+
+
+def enter(tab, front, crossed):
+    row = pl.BlockSpec((BLK, 16 * BLK), lambda step, tab_ref: (tab_ref[CROSS + step], 0))
+
+    def pick(step, tab_ref):
+        return (lax.max(tab_ref[GROUP + (1 - tab_ref[HALF]) * 8 + tab_ref[CROSS + step]], 0), 0, 0)
+
+    return pl.pallas_call(
+        enter_kernel,
+        out_shape=jax.ShapeDtypeStruct((8 * BLK, 16 * BLK), F32),
+        grid_spec=pltpu.PrefetchScalarGridSpec(
+            num_scalar_prefetch=1,
+            grid=(8,),
+            in_specs=[row, pl.BlockSpec((8, BLK, BLK), pick)],
+            out_specs=row,
+        ),
+        input_output_aliases={1: 0},
+        compiler_params=params(),
+        name="enter",
+    )(tab, front, crossed)
 
 
 def shift(value, axis, size, away):
@@ -409,22 +488,24 @@
     one_block = summed[:, 0].reshape(NPIV, BLK)
     lead_cols = summed[:, 1].reshape(NPIV, BLK)
 
-    along_z = [one_block] + [shift(one_block, ("zh", "zl"), 4, away) for away in range(1, 4)]
+    along_z = [shift(one_block, ("zh", "zl"), 4, away) for away in range(1, 4)]
     lead_pieces = gather_front(lead_cols, 3)
     moved = lax.ppermute(one_block, CUBE + FRONT, row_routes())
+    along_y = [one_block] + [shift(one_block, "y", 4, away) for away in range(1, 4)]
     along_z = jnp.stack(along_z)
-    col_pieces = [along_z]
+    deep = [along_z]
     for away in range(1, 4):
-        col_pieces.append(shift(along_z, "y", 4, away))
+        deep.append(shift(along_z, "y", 4, away))
     row_pieces = gather_front(moved)
     crossed = shift(arrived, "zh", 2, 1)
 
     inverse = lead_inverse(tab, lead_pieces)
-    cols = []
-    for away in range(4):
-        cols.append(col_panel(inverse, col_pieces[away]))
+    cols = [col_panel(inverse, along_y + [deep[0]])]
+    cols.append(col_panel(inverse, [deep[1], deep[3]]))
+    cols.append(col_panel(inverse, [deep[2]]))
     rows = row_panel(tab, inverse, row_pieces)
-    return finish(tab, parent_front, arrived, crossed, rows, cols)
+    schur = finish(tab, parent_front, arrived, rows, cols)
+    return enter(tab, schur, crossed)
 
 
 def solution(mesh):

time: 372 us -> 371 us (level); the launches traced: 371 us -> 363 us
  waiting for transfers between devices: 64.9 us -> 60.9 us
  Pallas kernels: 105 us -> 101 us
    ppermute x6, waiting for transfers between devices: 21.3 us -> 16.5 us  [gather_front(): lax.ppermute(block, 'x', [(i, (i + away) % 4) for i in range(sources)])]
    ppermute x15 -> x18, starting transfers between devices: 111 us -> 109 us  [shift(): lax.ppermute(value, axis, [(i, (i + away) % size) for i in range(size)])]
    ppermute x15 -> x18, waiting for transfers between devices: 15.4 us -> 16.2 us  [shift(): lax.ppermute(value, axis, [(i, (i + away) % size) for i in range(size)])]
  transfers between devices with their start and end apart: 23 -> 26, of which waited for: 12 -> 8; matrix products, arithmetic and copies ran while one was open for 0% -> 0% of each run, Pallas kernels for 20% -> 24%
where the time goes in v3:
time: 371 us; the launch traced here: 363 us
  starting transfers between devices  136 us (37%)
  Pallas kernels  101 us (27%)
  blocking collectives  61.1 us (16%)
  waiting for transfers between devices  60.9 us (16%)
    ppermute x18, starting transfers between devices, shift(): lax.ppermute(value, axis, [(i, (i + away) % size) for i in range(size)])  109 us
    all_to_all x1, blocking collectives, staged(): lax.all_to_all(packed, ('zl', 'y', 'x', 'core'), split_axis=0, concat_axi...  61.1 us
    pallas_call x1, Pallas kernels, lead_inverse(): pl.pallas_call(lead_kernel, out_shape=(jax.ShapeDtypeStruct((NPIV, NPIV),...  42.2 us
    all_to_all x1, waiting for transfers between devices, staged(): lax.all_to_all(strip, CUBE, split_axis=0, concat_axis=0, tiled=True)  28.2 us
    ppermute x6, starting transfers between devices, gather_front(): lax.ppermute(block, 'x', [(i, (i + away) % 4) for i in range(sources)])  19.7 us
    pallas_call x1, Pallas kernels, finish(): pl.pallas_call(finish_kernel, out_shape=jax.ShapeDtypeStruct((8 * BLK, 16...  19.3 us
    pallas_call x3, Pallas kernels, col_panel(): pl.pallas_call(col_kernel, out_shape=jax.ShapeDtypeStruct((2 * NPIV, coun...  16.8 us
    ppermute x6, waiting for transfers between devices, gather_front(): lax.ppermute(block, 'x', [(i, (i + away) % 4) for i in range(sources)])  16.5 us
  transfers between devices with their start and end apart: 26, of which 8 were waited for; matrix products, arithmetic and copies ran while one was open for 0% of the time, Pallas kernels for 24%

profile of v3, /device:TPU:0, one launch (start us, length us, event | category | flops | bytes accessed | tf_op | source)
XLA Modules:
  0.0 363.3 jit_solution(3438932252894658539)
XLA Ops:
  2.2 5.5 %pack_tiles.1 = f32[64,128,128]{2,1,0:T(8,128)} custom-call(s32[64]{0:T(128)} %make_table.1.tab_ref, f32[1024,1024]{1,0:T(8,128)} %odd_ref.1, f32[1024,1024]{1,0:T(8,128)} %odd_ref.1), custom_call_target="tpu_custom_call" | custom-call | tf_op jit(solution)/shard_map/pack_tiles/pallas_call | solution.py:88
  7.7 61.1 %all_to_all.10.tile_ref.own0.own1 = f32[64,128,128]{2,1,0:T(8,128)} all-to-all(f32[64,128,128]{2,1,0:T(8,128)} %pack_tiles.1), channel_id=1, replica_groups=mesh['zh'=2,'zl'=2,'y'=4,'x'=4,'core'=2] {'zl','y','x','core'}, dimensions={0} | all-to-all | bytes 8388608 | tf_op jit(solution)/shard_map/all_to_all | solution.py:483
  68.8 3.6 make_strip.1
  72.4 6.6 %all-to-all-start.1 = ((f32[16,2,128,128]{3,2,1,0:T(8,128)}), f32[16,2,128,128]{3,2,1,0:T(8,128)S(1)}, u32[]{:S(2)}, u32[]{:S(2)}) async-start(f32[16,2,128,128]{3,2,1,0:T(8,128)} %make_strip.1), calls=%async_computation.1 | async-start | bytes 4194304 | tf_op jit(solution)/shard_map/all_to_all | solution.py:486
  79.0 3.4 collective-permute-start.24
  82.4 28.2 %all-to-all-done.1 = f32[16,2,128,128]{3,2,1,0:T(8,128)S(1)} async-done(((f32[16,2,128,128]{3,2,1,0:T(8,128)}), f32[16,2,128,128]{3,2,1,0:T(8,128)S(1)}, u32[]{:S(2)}, u32[]{:S(2)}) %all-to-all-start.1) | async-done | bytes 2097184 | tf_op jit(solution)/shard_map/all_to_all | solution.py:486
  110.9 3.7 %collective-permute-start.2 = (f32[768,128]{1,0:T(8,128)S(1)}, f32[768,128]{1,0:T(8,128)S(1)}, u32[]{:S(2)}, u32[]{:S(2)}) collective-permute-start(f32[768,128]{1,0:T(8,128)S(1)} %bitcast.9), channel_id=1, source_target_pairs={{0,6},{2,0},{4,2},{1,7},{3,1},{5,3},{8,14},{10,8},{12,10},{9,15},{... | collective-permute-start | bytes 1179656 | tf_op jit(solution)/shard_map/ppermute | solution.py:465
  119.4 12.7 %collective-permute-done.2.refs_3_ = f32[768,128]{1,0:T(8,128)S(1)} collective-permute-done((f32[768,128]{1,0:T(8,128)S(1)}, f32[768,128]{1,0:T(8,128)S(1)}, u32[]{:S(2)}, u32[]{:S(2)}) %collective-permute-start.2) | collective-permute-done | bytes 393248 | tf_op jit(solution)/shard_map/ppermute | solution.py:465
  132.0 77.2 %collective-permute-start.19 = (f32[768,128]{1,0:T(8,128)S(1)}, f32[768,128]{1,0:T(8,128)S(1)}, u32[]{:S(2)}, u32[]{:S(2)}) collective-permute-start(f32[768,128]{1,0:T(8,128)S(1)} %bitcast.14), channel_id=1, source_target_pairs={{0,64},{32,96},{64,0},{96,32},{1,65},{33,97},{65,1},{97,33},{2,66}... | collective-permute-start | bytes 1179656 | tf_op jit(solution)/shard_map/ppermute | solution.py:459
  210.3 4.3 %collective-permute-start.16 = (f32[768,128]{1,0:T(8,128)S(1)}, f32[768,128]{1,0:T(8,128)}, u32[]{:S(2)}, u32[]{:S(2)}) collective-permute-start(f32[768,128]{1,0:T(8,128)S(1)} %bitcast.17), channel_id=1, source_target_pairs={{0,16},{8,24},{16,0},{24,8},{1,17},{9,25},{17,1},{25,9},{2,18},{10... | collective-permute-start | bytes 1179656 | tf_op jit(solution)/shard_map/ppermute | solution.py:459
  214.7 4.6 %collective-permute-done.19 = f32[768,128]{1,0:T(8,128)S(1)} collective-permute-done((f32[768,128]{1,0:T(8,128)S(1)}, f32[768,128]{1,0:T(8,128)S(1)}, u32[]{:S(2)}, u32[]{:S(2)}) %collective-permute-start.19) | collective-permute-done | bytes 393248 | tf_op jit(solution)/shard_map/ppermute | solution.py:459
  219.3 6.8 %collective-permute-done.18 = f32[768,128]{1,0:T(8,128)S(1)} collective-permute-done((f32[768,128]{1,0:T(8,128)S(1)}, f32[768,128]{1,0:T(8,128)S(1)}, u32[]{:S(2)}, u32[]{:S(2)}) %collective-permute-start.18) | collective-permute-done | bytes 393248 | tf_op jit(solution)/shard_map/ppermute | solution.py:459
  228.3 3.0 collective-permute-done.15.refs_1_
  231.4 10.7 %collective-permute-start.10 = (f32[768,128]{1,0:T(8,128)S(1)}, f32[768,128]{1,0:T(8,128)S(1)}, u32[]{:S(2)}, u32[]{:S(2)}) collective-permute-start(f32[768,128]{1,0:T(8,128)S(1)} %collective-permute-done.7.refs_0_), channel_id=1, source_target_pairs={{0,6},{2,0},{4,2},{6,4},{1,7},{3,1},{5,3},{7,5},{8,14},{10,8},{12,... | collective-permute-start | bytes 1179656 | tf_op jit(solution)/shard_map/ppermute | solution.py:465
  242.0 4.7 %collective-permute-start.11 = (f32[768,128]{1,0:T(8,128)S(1)}, f32[768,128]{1,0:T(8,128)S(1)}, u32[]{:S(2)}, u32[]{:S(2)}) collective-permute-start(f32[768,128]{1,0:T(8,128)S(1)} %collective-permute-done.7.refs_0_), channel_id=1, source_target_pairs={{0,1},{1,0},{2,3},{3,2},{4,5},{5,4},{6,7},{7,6},{8,9},{9,8},{10,11... | collective-permute-start | bytes 1179656 | tf_op jit(solution)/shard_map/ppermute | solution.py:459
  248.9 11.1 %collective-permute-start.14 = (f32[768,128]{1,0:T(8,128)S(1)}, f32[768,128]{1,0:T(8,128)S(1)}, u32[]{:S(2)}, u32[]{:S(2)}) collective-permute-start(f32[768,128]{1,0:T(8,128)S(1)} %collective-permute-done.10.refs_3_), channel_id=1, source_target_pairs={{0,1},{1,0},{2,3},{3,2},{4,5},{5,4},{6,7},{7,6},{8,9},{9,8},{10,11... | collective-permute-start | bytes 1179656 | tf_op jit(solution)/shard_map/ppermute | solution.py:459
  260.2 4.5 %collective-permute-start.23 = (f32[3,768,128]{2,1,0:T(8,128)S(1)}, f32[3,768,128]{2,1,0:T(8,128)S(1)}, u32[]{:S(2)}, u32[]{:S(2)}) collective-permute-start(f32[3,768,128]{2,1,0:T(8,128)S(1)} %pad_maximum_fusion.refs_4_), channel_id=1, source_target_pairs={{0,16},{8,24},{16,0},{24,8},{1,17},{9,25},{17,1},{25,9},{2,18},{10... | collective-permute-start | bytes 3538952 | tf_op jit(solution)/shard_map/ppermute | solution.py:459
  269.9 42.2 %lead_inverse.1 = (bf16[768,768]{1,0:T(8,128)(2,1)}, bf16[768,768]{1,0:T(8,128)(2,1)}) custom-call(s32[64]{0:T(128)} %make_table.1.tab_ref, f32[768,128]{1,0:T(8,128)} %bitcast.12, f32[768,128]{1,0:T(8,128)} %copy-done.16, f32[768,128]{1,0:T(8,128)} %copy-done.15, f32[768,128]{1,0:T(8,128)} %copy-done.14, f32[768,128]{1,0:T(8,128)} %copy-done.13, ...), custom_call_target="tpu_custom_call" | custom-call | tf_op jit(solution)/shard_map/lead_inverse/pallas_call | solution.py:251
  312.2 6.7 %col_panel.3.refs_0_ = bf16[1536,896]{1,0:T(8,128)(2,1)} custom-call(bf16[768,768]{1,0:T(8,128)(2,1)} %get-tuple-element.7.high_in, bf16[768,768]{1,0:T(8,128)(2,1)} %get-tuple-element.8.low_in, f32[768,128]{1,0:T(8,128)} %bitcast.20, f32[768,128]{1,0:T(8,128)} %collective-permute-done.15.refs_1_, f32[768,128]{1,0:T(8,128)} %collective-permute-done.16.refs_2_, ...), custom_call_target="tpu_custom_call" | custom-call | tf_op jit(solution)/shard_map/col_panel/pallas_call | solution.py:307
  318.9 7.7 %row_panel.1.rows_ref = f32[1024,768]{1,0:T(8,128)} custom-call(s32[64]{0:T(128)} %make_table.1.tab_ref, bf16[768,768]{1,0:T(8,128)(2,1)} %get-tuple-element.7.high_in, bf16[768,768]{1,0:T(8,128)(2,1)} %get-tuple-element.8.low_in, f32[768,128]{1,0:T(8,128)} %copy-done.6, f32[768,128]{1,0:T(8,128)} %copy-done.10, f32[768,128]{1,0:T(8,128)} %copy-done.9, ...), custom_call_target="tpu_custom_call" | custom-call | tf_op jit(solution)/shard_map/row_panel/pallas_call | solution.py:329
  327.6 4.4 %col_panel.5.refs_2_ = bf16[1536,384]{1,0:T(8,128)(2,1)} custom-call(bf16[768,768]{1,0:T(8,128)(2,1)} %get-tuple-element.7.high_in, bf16[768,768]{1,0:T(8,128)(2,1)} %get-tuple-element.8.low_in, f32[3,768,128]{2,1,0:T(8,128)} %copy-done.5), custom_call_target="tpu_custom_call" | custom-call | tf_op jit(solution)/shard_map/col_panel/pallas_call | solution.py:307
  334.1 5.7 %col_panel.4.refs_1_ = bf16[1536,768]{1,0:T(8,128)(2,1)} custom-call(bf16[768,768]{1,0:T(8,128)(2,1)} %get-tuple-element.7.high_in, bf16[768,768]{1,0:T(8,128)(2,1)} %get-tuple-element.8.low_in, f32[3,768,128]{2,1,0:T(8,128)} %copy-done.4, f32[3,768,128]{2,1,0:T(8,128)} %copy-done.3), custom_call_target="tpu_custom_call" | custom-call | tf_op jit(solution)/shard_map/col_panel/pallas_call | solution.py:307
  339.8 19.3 %finish.1.front_ref = f32[1024,2048]{1,0:T(8,128)} custom-call(s32[64]{0:T(128)} %make_table.1.tab_ref, f32[1024,2048]{1,0:T(8,128)} %parent_ref.3, f32[64,128,128]{2,1,0:T(8,128)} %all_to_all.10.tile_ref.own0.own1, f32[64,128,128]{2,1,0:T(8,128)} %all_to_all.10.tile_ref.own0.own1, f32[1024,768]{1,0:T(8,128)} %row_panel.1.rows_ref, ...), custom_call_target="tpu_custom_call" | custom-call | tf_op jit(solution)/shard_map/finish/pallas_call | solution.py:401
  359.1 4.1 %enter.1 = f32[1024,2048]{1,0:T(8,128)} custom-call(s32[64]{0:T(128)} %make_table.1.tab_ref, f32[1024,2048]{1,0:T(8,128)} %finish.1.front_ref, f32[64,128,128]{2,1,0:T(8,128)} %collective-permute-done.24.tile_ref), custom_call_target="tpu_custom_call", output_to_operand_aliasing={{}: (1, {})} | custom-call | tf_op jit(solution)/shard_map/enter/pallas_call | solution.py:443
  (83 shorter events, 21.0 us)
Async XLA Ops:
  72.4 38.2 %all-to-all-start.1 = ((f32[16,2,128,128]{3,2,1,0:T(8,128)}), f32[16,2,128,128]{3,2,1,0:T(8,128)S(1)}, u32[]{:S(2)}, u32[]{:S(2)}) async-start(f32[16,2,128,128]{3,2,1,0:T(8,128)} %make_strip.1), calls=%async_computation.1 | async-start | bytes 4194304 | tf_op jit(solution)/shard_map/all_to_all | solution.py:486
  79.0 280.2 %collective-permute-start.24 = (f32[64,128,128]{2,1,0:T(8,128)}, f32[64,128,128]{2,1,0:T(8,128)}, u32[]{:S(2)}, u32[]{:S(2)}) collective-permute-start(f32[64,128,128]{2,1,0:T(8,128)} %all_to_all.10.tile_ref.own0.own1), channel_id=1, source_target_pairs={{0,64},{64,0},{1,65},{65,1},{2,66},{66,2},{3,67},{67,3},{4,68},{68... | collective-permute-start | bytes 12582920 | tf_op jit(solution)/shard_map/ppermute | solution.py:459
  110.8 7.9 %collective-permute-start.3 = (f32[768,128]{1,0:T(8,128)S(1)}, f32[768,128]{1,0:T(8,128)S(1)}, u32[]{:S(2)}, u32[]{:S(2)}) collective-permute-start(f32[768,128]{1,0:T(8,128)S(1)} %bitcast.8), channel_id=1, source_target_pairs={{0,1},{1,0},{2,3},{3,2},{4,5},{5,4},{6,7},{7,6},{8,9},{9,8},{10,11... | collective-permute-start | bytes 1179656 | tf_op jit(solution)/shard_map/ppermute | solution.py:459
  110.9 21.2 %collective-permute-start.2 = (f32[768,128]{1,0:T(8,128)S(1)}, f32[768,128]{1,0:T(8,128)S(1)}, u32[]{:S(2)}, u32[]{:S(2)}) collective-permute-start(f32[768,128]{1,0:T(8,128)S(1)} %bitcast.9), channel_id=1, source_target_pairs={{0,6},{2,0},{4,2},{1,7},{3,1},{5,3},{8,14},{10,8},{12,10},{9,15},{... | collective-permute-start | bytes 1179656 | tf_op jit(solution)/shard_map/ppermute | solution.py:465
  114.6 94.7 %collective-permute-start.1 = (f32[768,128]{1,0:T(8,128)S(1)}, f32[768,128]{1,0:T(8,128)S(1)}, u32[]{:S(2)}, u32[]{:S(2)}) collective-permute-start(f32[768,128]{1,0:T(8,128)S(1)} %bitcast.10), channel_id=1, source_target_pairs={{0,4},{2,6},{4,0},{1,5},{3,7},{5,1},{8,12},{10,14},{12,8},{9,13},{... | collective-permute-start | bytes 1179656 | tf_op jit(solution)/shard_map/ppermute | solution.py:465
  117.3 93.0 %collective-permute-start = (f32[768,128]{1,0:T(8,128)S(1)}, f32[768,128]{1,0:T(8,128)S(1)}, u32[]{:S(2)}, u32[]{:S(2)}) collective-permute-start(f32[768,128]{1,0:T(8,128)S(1)} %bitcast.11), channel_id=1, source_target_pairs={{0,2},{2,4},{4,6},{1,3},{3,5},{5,7},{8,10},{10,12},{12,14},{9,11},... | collective-permute-start | bytes 1179656 | tf_op jit(solution)/shard_map/ppermute | solution.py:465
  118.7 91.6 %collective-permute-start.20 = (f32[768,128]{1,0:T(8,128)S(1)}, f32[768,128]{1,0:T(8,128)S(1)}, u32[]{:S(2)}, u32[]{:S(2)}) collective-permute-start(f32[768,128]{1,0:T(8,128)S(1)} %bitcast.13), channel_id=1, source_target_pairs={{0,96},{32,0},{64,32},{96,64},{1,97},{33,1},{65,33},{97,65},{2,98}... | collective-permute-start | bytes 1179656 | tf_op jit(solution)/shard_map/ppermute | solution.py:459
  132.0 87.2 %collective-permute-start.19 = (f32[768,128]{1,0:T(8,128)S(1)}, f32[768,128]{1,0:T(8,128)S(1)}, u32[]{:S(2)}, u32[]{:S(2)}) collective-permute-start(f32[768,128]{1,0:T(8,128)S(1)} %bitcast.14), channel_id=1, source_target_pairs={{0,64},{32,96},{64,0},{96,32},{1,65},{33,97},{65,1},{97,33},{2,66}... | collective-permute-start | bytes 1179656 | tf_op jit(solution)/shard_map/ppermute | solution.py:459
  209.3 16.8 %collective-permute-start.18 = (f32[768,128]{1,0:T(8,128)S(1)}, f32[768,128]{1,0:T(8,128)S(1)}, u32[]{:S(2)}, u32[]{:S(2)}) collective-permute-start(f32[768,128]{1,0:T(8,128)S(1)} %bitcast.15), channel_id=1, source_target_pairs={{0,32},{32,64},{64,96},{96,0},{1,33},{33,65},{65,97},{97,1},{2,34}... | collective-permute-start | bytes 1179656 | tf_op jit(solution)/shard_map/ppermute | solution.py:459
  210.3 16.5 %collective-permute-start.17 = (f32[768,128]{1,0:T(8,128)S(1)}, f32[768,128]{1,0:T(8,128)}, u32[]{:S(2)}, u32[]{:S(2)}) collective-permute-start(f32[768,128]{1,0:T(8,128)S(1)} %bitcast.16), channel_id=1, source_target_pairs={{0,24},{8,0},{16,8},{24,16},{1,25},{9,1},{17,9},{25,17},{2,26},{10... | collective-permute-start | bytes 1179656 | tf_op jit(solution)/shard_map/ppermute | solution.py:459
  210.3 17.9 %collective-permute-start.16 = (f32[768,128]{1,0:T(8,128)S(1)}, f32[768,128]{1,0:T(8,128)}, u32[]{:S(2)}, u32[]{:S(2)}) collective-permute-start(f32[768,128]{1,0:T(8,128)S(1)} %bitcast.17), channel_id=1, source_target_pairs={{0,16},{8,24},{16,0},{24,8},{1,17},{9,25},{17,1},{25,9},{2,18},{10... | collective-permute-start | bytes 1179656 | tf_op jit(solution)/shard_map/ppermute | solution.py:459
  219.3 12.1 %collective-permute-start.15 = (f32[768,128]{1,0:T(8,128)S(1)}, f32[768,128]{1,0:T(8,128)}, u32[]{:S(2)}, u32[]{:S(2)}) collective-permute-start(f32[768,128]{1,0:T(8,128)S(1)} %bitcast.18), channel_id=1, source_target_pairs={{0,8},{8,16},{16,24},{24,0},{1,9},{9,17},{17,25},{25,1},{2,10},{10... | collective-permute-start | bytes 1179656 | tf_op jit(solution)/shard_map/ppermute | solution.py:459
  226.8 15.2 %collective-permute-start.6 = (f32[768,128]{1,0:T(8,128)S(1)}, f32[768,128]{1,0:T(8,128)S(1)}, u32[]{:S(2)}, u32[]{:S(2)}) collective-permute-start(f32[768,128]{1,0:T(8,128)S(1)} %collective-permute-done.2.refs_3_), channel_id=1, source_target_pairs={{0,1},{1,0},{2,3},{3,2},{4,5},{5,4},{6,7},{7,6},{8,9},{9,8},{10,11... | collective-permute-start | bytes 1179656 | tf_op jit(solution)/shard_map/ppermute | solution.py:459
  228.2 18.5 %collective-permute-start.5 = (f32[768,128]{1,0:T(8,128)S(1)}, f32[768,128]{1,0:T(8,128)S(1)}, u32[]{:S(2)}, u32[]{:S(2)}) collective-permute-start(f32[768,128]{1,0:T(8,128)S(1)} %collective-permute-done.1.refs_2_), channel_id=1, source_target_pairs={{0,1},{1,0},{2,3},{3,2},{4,5},{5,4},{6,7},{7,6},{8,9},{9,8},{10,11... | collective-permute-start | bytes 1179656 | tf_op jit(solution)/shard_map/ppermute | solution.py:459
  231.4 15.4 %collective-permute-start.4 = (f32[768,128]{1,0:T(8,128)S(1)}, f32[768,128]{1,0:T(8,128)S(1)}, u32[]{:S(2)}, u32[]{:S(2)}) collective-permute-start(f32[768,128]{1,0:T(8,128)S(1)} %collective-permute-done.refs_1_), channel_id=1, source_target_pairs={{0,1},{1,0},{2,3},{3,2},{4,5},{5,4},{6,7},{7,6},{8,9},{9,8},{10,11... | collective-permute-start | bytes 1179656 | tf_op jit(solution)/shard_map/ppermute | solution.py:459
  231.4 17.6 %collective-permute-start.10 = (f32[768,128]{1,0:T(8,128)S(1)}, f32[768,128]{1,0:T(8,128)S(1)}, u32[]{:S(2)}, u32[]{:S(2)}) collective-permute-start(f32[768,128]{1,0:T(8,128)S(1)} %collective-permute-done.7.refs_0_), channel_id=1, source_target_pairs={{0,6},{2,0},{4,2},{6,4},{1,7},{3,1},{5,3},{7,5},{8,14},{10,8},{12,... | collective-permute-start | bytes 1179656 | tf_op jit(solution)/shard_map/ppermute | solution.py:465
  242.0 18.2 %collective-permute-start.11 = (f32[768,128]{1,0:T(8,128)S(1)}, f32[768,128]{1,0:T(8,128)S(1)}, u32[]{:S(2)}, u32[]{:S(2)}) collective-permute-start(f32[768,128]{1,0:T(8,128)S(1)} %collective-permute-done.7.refs_0_), channel_id=1, source_target_pairs={{0,1},{1,0},{2,3},{3,2},{4,5},{5,4},{6,7},{7,6},{8,9},{9,8},{10,11... | collective-permute-start | bytes 1179656 | tf_op jit(solution)/shard_map/ppermute | solution.py:459
  246.7 18.0 %collective-permute-start.9 = (f32[768,128]{1,0:T(8,128)S(1)}, f32[768,128]{1,0:T(8,128)S(1)}, u32[]{:S(2)}, u32[]{:S(2)}) collective-permute-start(f32[768,128]{1,0:T(8,128)S(1)} %collective-permute-done.7.refs_0_), channel_id=1, source_target_pairs={{0,4},{2,6},{4,0},{6,2},{1,5},{3,7},{5,1},{7,3},{8,12},{10,14},{12... | collective-permute-start | bytes 1179656 | tf_op jit(solution)/shard_map/ppermute | solution.py:465
  246.7 20.8 %collective-permute-start.8 = (f32[768,128]{1,0:T(8,128)S(1)}, f32[768,128]{1,0:T(8,128)S(1)}, u32[]{:S(2)}, u32[]{:S(2)}) collective-permute-start(f32[768,128]{1,0:T(8,128)S(1)} %collective-permute-done.7.refs_0_), channel_id=1, source_target_pairs={{0,2},{2,4},{4,6},{6,0},{1,3},{3,5},{5,7},{7,1},{8,10},{10,12},{12... | collective-permute-start | bytes 1179656 | tf_op jit(solution)/shard_map/ppermute | solution.py:465
  248.9 19.1 %collective-permute-start.14 = (f32[768,128]{1,0:T(8,128)S(1)}, f32[768,128]{1,0:T(8,128)S(1)}, u32[]{:S(2)}, u32[]{:S(2)}) collective-permute-start(f32[768,128]{1,0:T(8,128)S(1)} %collective-permute-done.10.refs_3_), channel_id=1, source_target_pairs={{0,1},{1,0},{2,3},{3,2},{4,5},{5,4},{6,7},{7,6},{8,9},{9,8},{10,11... | collective-permute-start | bytes 1179656 | tf_op jit(solution)/shard_map/ppermute | solution.py:459
  260.2 66.4 %collective-permute-start.23 = (f32[3,768,128]{2,1,0:T(8,128)S(1)}, f32[3,768,128]{2,1,0:T(8,128)S(1)}, u32[]{:S(2)}, u32[]{:S(2)}) collective-permute-start(f32[3,768,128]{2,1,0:T(8,128)S(1)} %pad_maximum_fusion.refs_4_), channel_id=1, source_target_pairs={{0,16},{8,24},{16,0},{24,8},{1,17},{9,25},{17,1},{25,9},{2,18},{10... | collective-permute-start | bytes 3538952 | tf_op jit(solution)/shard_map/ppermute | solution.py:459
  264.7 67.3 %collective-permute-start.22 = (f32[3,768,128]{2,1,0:T(8,128)S(1)}, f32[3,768,128]{2,1,0:T(8,128)S(1)}, u32[]{:S(2)}, u32[]{:S(2)}) collective-permute-start(f32[3,768,128]{2,1,0:T(8,128)S(1)} %pad_maximum_fusion.refs_4_), channel_id=1, source_target_pairs={{0,24},{8,0},{16,8},{24,16},{1,25},{9,1},{17,9},{25,17},{2,26},{10... | collective-permute-start | bytes 3538952 | tf_op jit(solution)/shard_map/ppermute | solution.py:459
  267.6 64.5 %collective-permute-start.21 = (f32[3,768,128]{2,1,0:T(8,128)S(1)}, f32[3,768,128]{2,1,0:T(8,128)S(1)}, u32[]{:S(2)}, u32[]{:S(2)}) collective-permute-start(f32[3,768,128]{2,1,0:T(8,128)S(1)} %pad_maximum_fusion.refs_4_), channel_id=1, source_target_pairs={{0,8},{8,16},{16,24},{24,0},{1,9},{9,17},{17,25},{25,1},{2,10},{10... | collective-permute-start | bytes 3538952 | tf_op jit(solution)/shard_map/ppermute | solution.py:459
  269.8 49.1 %collective-permute-start.12 = (f32[768,128]{1,0:T(8,128)S(1)}, f32[768,128]{1,0:T(8,128)}, u32[]{:S(2)}, u32[]{:S(2)}) collective-permute-start(f32[768,128]{1,0:T(8,128)S(1)} %collective-permute-done.8.refs_1_), channel_id=1, source_target_pairs={{0,1},{1,0},{2,3},{3,2},{4,5},{5,4},{6,7},{7,6},{8,9},{9,8},{10,11... | collective-permute-start | bytes 1179656 | tf_op jit(solution)/shard_map/ppermute | solution.py:459
  (22 other events, 1259.7 us)
